TPU v7x, 256 devices: a whole 4x4x8 slice. The times are simulated.
256 devices in a mesh: ctx: 32 (over z, x), tp: 8 (over y, core).
Axes of the slice: x: 4, y: 4, z: 8, core: 2. Of those that a mesh axis runs over, the one named last changes fastest.
Arguments:
- tokens: bfloat16 [24576, 4096], P('ctx'), may hold values from -6 to 6
- qkv_weight: bfloat16 [3, 4096, 4096], P(None, 'ctx', 'tp'), may hold values from -0.09375 to 0.09375
- short_filter: float32 [3, 7, 4096], P(None, None, 'tp'), may hold values from -2.4 to 2.4
- long_filter: float32 [256, 128], P('tp'), may hold values from -0.9 to 0.9
- decay_rate: float32 [256], P('tp'), may hold values from 0.004 to 0.2
- skip_gain: float32 [4096], P('tp'), may hold values from -3 to 3
- out_weight: bfloat16 [4096, 4096], P('tp', 'ctx'), may hold values from -0.09375 to 0.09375
Outputs:
- block_out: bfloat16 [24576, 4096], P(('ctx', 'tp'))
All inputs are finite; a program needn't handle non-finite values.
Results may differ from a plain program's by a relative error of at most 0.008.
Values may be sent and summed in bfloat16 or wider, within the bound.
A program may use at most 64 MiB of HBM per device.

v0:
```python
import jax
import jax.numpy as jnp
from jax import lax
from jax.sharding import PartitionSpec as P


def short_conv(extended, short_filter):
    span = short_filter.shape[1]
    length = extended.shape[2] - (span - 1)
    result = short_filter[:, 0, :, None] * extended[:, :, span - 1 :]
    for offset in range(1, span):
        start = span - 1 - offset
        result = result + short_filter[:, offset, :, None] * extended[:, :, start : start + length]
    return result


def banded(filters):
    tap_count = filters.shape[1]
    row_index = jnp.arange(tap_count)[:, None]
    col_index = jnp.arange(tap_count)[None, :]
    distance = (row_index - col_index) % tap_count
    picker = (distance[None, :, :] == jnp.arange(tap_count)[:, None, None]).astype(jnp.bfloat16)
    full_band = jnp.einsum("gk,kij->gij", filters, picker, preferred_element_type=jnp.float32)
    lower_part = row_index >= col_index
    lower_band = jnp.where(lower_part[None], full_band, 0.0).astype(jnp.bfloat16)
    upper_band = jnp.where(lower_part[None], 0.0, full_band).astype(jnp.bfloat16)
    return (lower_band, upper_band)


def long_mix(features, gated, previous, filters, gain):
    channel_count, length = gated.shape
    tap_count = filters.shape[1]
    group_count = filters.shape[0]
    extended = jnp.concatenate([previous, gated], axis=1)
    blocks = extended.reshape(
        group_count, channel_count // group_count, length // tap_count + 1, tap_count
    )
    lower_band, upper_band = banded(filters)
    current = jnp.einsum(
        "gij,gcbj->gcbi", lower_band, blocks[:, :, 1:], preferred_element_type=jnp.float32
    )
    current = current + jnp.einsum(
        "gij,gcbj->gcbi", upper_band, blocks[:, :, :-1], preferred_element_type=jnp.float32
    )
    filtered = current.reshape(channel_count, length)
    return (features[0] * (filtered + gain[:, None] * gated.astype(jnp.float32))).astype(
        jnp.bfloat16
    )


def per_device(tokens, qkv_weight, short_filter, long_filter, decay_rate, skip_gain, out_weight):
    local_width = qkv_weight.shape[2]
    tap_count = long_filter.shape[1]
    span = short_filter.shape[1]
    group_width = local_width // long_filter.shape[0]
    projected = jnp.einsum(
        "tr,src->sct",
        tokens,
        lax.all_gather(qkv_weight, "ctx", axis=1, tiled=True),
        preferred_element_type=jnp.float32,
    )
    qkv = projected.astype(jnp.bfloat16)
    tap_index = jnp.arange(tap_count, dtype=jnp.float32)
    filters = (long_filter * jnp.exp(-decay_rate[:, None] * tap_index[None, :])).astype(
        jnp.bfloat16
    )
    moved = lax.all_to_all(qkv, "ctx", split_axis=1, concat_axis=2, tiled=True)
    share = moved.shape[1]
    position = lax.axis_index("ctx")
    part_short = lax.dynamic_slice_in_dim(short_filter, position * share, share, 2)
    part_filters = lax.dynamic_slice_in_dim(
        filters, position * (share // group_width), share // group_width, 0
    )
    part_gain = lax.dynamic_slice_in_dim(skip_gain, position * share, share, 0)
    leading = jnp.zeros((3, share, span - 1), jnp.bfloat16)
    features = short_conv(jnp.concatenate([leading, moved], axis=2), part_short)
    gated = (features[1] * features[2]).astype(jnp.bfloat16)
    previous = jnp.zeros((share, tap_count), jnp.bfloat16)
    regrouped = long_mix(features, gated, previous, part_filters, part_gain)
    mixed = lax.all_to_all(regrouped, "ctx", split_axis=1, concat_axis=0, tiled=True)
    out_rows = lax.all_gather(out_weight, "ctx", axis=1, tiled=True)
    summed = lax.psum_scatter(
        lax.dot_general(
            mixed, out_rows, (((0,), (0,)), ((), ())), preferred_element_type=jnp.float32
        ),
        "tp",
        scatter_dimension=0,
        tiled=True,
    )
    return summed.astype(jnp.bfloat16)


def solution(mesh):
    in_specs = (
        P("ctx", None),
        P(None, "ctx", "tp"),
        P(None, None, "tp"),
        P("tp", None),
        P("tp"),
        P("tp"),
        P("tp", "ctx"),
    )
    out_specs = P(("ctx", "tp"), None)
    return jax.shard_map(
        per_device, mesh=mesh, in_specs=in_specs, out_specs=out_specs, check_vma=False
    )
```

profile of v0, /device:TPU:1, one launch (start us, length us, event | category | flops | bytes accessed | tf_op | source)
XLA Modules:
  0.0 379.6 jit_solution(5646571431311405019)
XLA Ops:
  6.5 1.9 copy.14
  8.5 127.2 %all-gather.3.cloned.1.call-done = bf16[3,4096,512]{1,2,0:T(8,128)(2,1)} async-done(((bf16[3,128,512]{1,2,0:T(8,128)(2,1)}), bf16[3,4096,512]{1,2,0:T(8,128)(2,1)}) %all-gather.3.cloned.1.call-update) | async-done | bytes 12582928 | tf_op jit(solution)/shard_map/all_gather | solution.py:59
  135.6 14.8 %fusion.4 = bf16[3,512,768]{2,1,0:T(8,128)(2,1)S(1)} fusion(bf16[3,4096,512]{1,2,0:T(8,128)(2,1)} %all-gather.3.cloned.1.call-done, bf16[768,4096]{1,0:T(8,128)(2,1)} %param.7), kind=kOutput, calls=%fused_computation.11 | convolution fusion | flops 9664856064 | bytes 21233664 | tf_op jit(solution)/shard_map/tr,src->sct/dot_general | solution.py:56
  150.4 3.7 copy.15
  154.1 6.8 %all-to-all-start = ((bf16[3,512,768]{2,0,1:T(4,128)(2,1)}), bf16[3,512,768]{2,0,1:T(4,128)(2,1)S(1)}, u32[]{:S(2)}, u32[]{:S(2)}) async-start(bf16[3,512,768]{2,0,1:T(4,128)(2,1)} %copy.15), calls=%async_computation | async-start | bytes 6291456 | tf_op jit(solution)/shard_map/all_to_all | solution.py:67
  160.9 0.2 all-gather.5.cloned.1.call-start
  161.1 0.5 all-gather.5.cloned.1.call-update
  161.6 1.1 constant_dynamic-slice_fusion.5
  162.7 0.8 dynamic_slice.11
  163.5 0.6 dynamic-slice.7
  164.1 1.2 iota_compare_fusion
  165.4 3.5 fusion
  168.8 66.1 %all-to-all-done = bf16[3,512,768]{2,0,1:T(4,128)(2,1)S(1)} async-done(((bf16[3,512,768]{2,0,1:T(4,128)(2,1)}), bf16[3,512,768]{2,0,1:T(4,128)(2,1)S(1)}, u32[]{:S(2)}, u32[]{:S(2)}) %all-to-all-start) | async-done | bytes 2359328 | tf_op jit(solution)/shard_map/all_to_all | solution.py:67
  234.9 3.1 copy.50
  238.0 3.0 all_to_all.28
  241.1 4.9 %multiply_add_fusion = f32[3,16,24576]{2,1,0:T(8,128)S(1)} fusion(bf16[3,16,24576]{2,1,0:T(8,128)(2,1)S(1)} %all_to_all.28, f32[3,16]{1,0:T(4,128)S(1)} %get-tuple-element.14, f32[3,16]{1,0:T(4,128)S(1)} %get-tuple-element.15, f32[3,16]{1,0:T(4,128)S(1)} %get-tuple-element.16, f32[3,16]{1,0:T(4,128)S(1)} %get-tuple-element.17, ...), kind=kLoop, calls=%fused_computation.5 | loop fusion | flops 23592960 | bytes 7079232 | tf_op jit(solution)/shard_map/add | solution.py:13
  245.9 0.2 fusion.7
  246.2 1.0 concatenate.7
  247.1 1.5 reshape.79
  248.7 0.4 fusion.9
  249.0 1.5 convolution_add_fusion
  250.6 2.6 reshape.83
  253.2 0.5 copy.29
  253.7 0.2 copy.30
  253.8 0.8 copy-done
  254.7 3.4 fusion.8
  258.0 6.4 %all-to-all-start.1 = ((bf16[16,32,768]{2,0,1:T(8,128)(2,1)}), bf16[16,32,768]{2,0,1:T(8,128)(2,1)S(1)}, u32[]{:S(2)}, u32[]{:S(2)}) async-start(bf16[16,32,768]{2,0,1:T(8,128)(2,1)} %fusion.8), calls=%async_computation.1 | async-start | bytes 1572864 | tf_op jit(solution)/shard_map/all_to_all | solution.py:80
  264.5 7.9 %all-gather.5.cloned.1.call-done = bf16[512,4096]{1,0:T(8,128)(2,1)} async-done(((bf16[512,128]{1,0:T(8,128)(2,1)}), bf16[512,4096]{1,0:T(8,128)(2,1)}) %all-gather.5.cloned.1.call-update) | async-done | bytes 4194320 | tf_op jit(solution)/shard_map/all_gather | solution.py:81
  272.4 15.2 %all-to-all-done.1 = bf16[16,32,768]{2,0,1:T(8,128)(2,1)S(1)} async-done(((bf16[16,32,768]{2,0,1:T(8,128)(2,1)}), bf16[16,32,768]{2,0,1:T(8,128)(2,1)S(1)}, u32[]{:S(2)}, u32[]{:S(2)}) %all-to-all-start.1) | async-done | bytes 786464 | tf_op jit(solution)/shard_map/all_to_all | solution.py:80
  287.6 8.5 %fusion.29 = f32[768,4096]{1,0:T(8,128)} fusion(bf16[512,768]{1,0:T(8,128)(2,1)S(1)} %bitcast.66, bf16[512,4096]{1,0:T(8,128)(2,1)} %all-gather.5.cloned.1.call-done), kind=kOutput, calls=%fused_computation.59 | convolution fusion | flops 3221225472 | bytes 17563648 | tf_op jit(solution)/shard_map/dot_general | solution.py:83
  296.2 74.5 %reduce-scatter.2.cloned.1.call-done = f32[96,4096]{1,0:T(8,128)} async-done(((f32[768,4096]{1,0:T(8,128)}), f32[96,4096]{1,0:T(8,128)}) %reduce-scatter.2.cloned.1.call-update) | async-done | bytes 1572880 | tf_op jit(solution)/shard_map/reduce_scatter | solution.py:82
  370.7 2.4 convert_element_type.74
  (13 shorter events, 0.1 us)
Async XLA Ops:
  6.5 129.1 %all-gather.3.cloned.1.call-start = ((), (), s32[]{:S(2)}) async-start(), calls=%async_computation.3 | async-start | bytes 12976128 | tf_op jit(solution)/shard_map/all_gather | solution.py:59
  154.1 8.6 %copy-start.1 = (f32[32]{0:T(128)S(1)}, f32[32]{0:T(128)}, u32[]{:S(2)}) copy-start(f32[32]{0:T(128)} %param.11) | copy-start | bytes 388
  154.1 80.8 %all-to-all-start = ((bf16[3,512,768]{2,0,1:T(4,128)(2,1)}), bf16[3,512,768]{2,0,1:T(4,128)(2,1)S(1)}, u32[]{:S(2)}, u32[]{:S(2)}) async-start(bf16[3,512,768]{2,0,1:T(4,128)(2,1)} %copy.15), calls=%async_computation | async-start | bytes 6291456 | tf_op jit(solution)/shard_map/all_to_all | solution.py:67
  160.9 111.6 %all-gather.5.cloned.1.call-start = ((), (), s32[]{:S(2)}) async-start(), calls=%async_computation.4 | async-start | bytes 4325376 | tf_op jit(solution)/shard_map/all_gather | solution.py:81
  253.2 1.5 copy-start
  258.0 29.6 %all-to-all-start.1 = ((bf16[16,32,768]{2,0,1:T(8,128)(2,1)}), bf16[16,32,768]{2,0,1:T(8,128)(2,1)S(1)}, u32[]{:S(2)}, u32[]{:S(2)}) async-start(bf16[16,32,768]{2,0,1:T(8,128)(2,1)} %fusion.8), calls=%async_computation.1 | async-start | bytes 1572864 | tf_op jit(solution)/shard_map/all_to_all | solution.py:80
  264.5 106.2 %reduce-scatter.2.cloned.1.call-start = ((), (), s32[]{:S(2)}) async-start(), calls=%async_computation.5 | async-start | bytes 14155776 | tf_op jit(solution)/shard_map/reduce_scatter | solution.py:82
Sparse Core Ops, SparseCore 0:
  9.8 125.8 all-gather.2
  164.1 108.2 all-gather.4
  296.3 74.2 reduce-scatter.1
where the time goes:
time: 380 us
  waiting for transfers between devices  291 us (77%)
  matrix products  28.7 us (8%)
  local copies, waits for them, and re-layouts  20.7 us (5%)
  starting transfers between devices  13.5 us (4%)
  between operations  13.2 us (3%)
  other arithmetic  12.2 us (3%)
    all_gather x1, waiting for transfers between devices, per_device(): lax.all_gather(qkv_weight, 'ctx', axis=1, tiled=True)  127 us
    reduce_scatter x1, waiting for transfers between devices, per_device(): lax.psum_scatter(lax.dot_general(mixed, out_rows, (((0,), (0,)), ((), ())...  74.5 us
    all_to_all x1, waiting for transfers between devices, per_device(): moved = lax.all_to_all(qkv, 'ctx', split_axis=1, concat_axis=2, tiled=True)  66.1 us
    all_to_all x1, waiting for transfers between devices, per_device(): lax.all_to_all(regrouped, 'ctx', split_axis=1, concat_axis=0, tiled=True)  15.2 us
    dot_general x1, matrix products, per_device(): jnp.einsum('tr,src->sct', tokens, lax.all_gather(qkv_weight, 'ctx', axis=...  14.8 us
    dot_general x1, matrix products, per_device(): lax.dot_general(mixed, out_rows, (((0,), (0,)), ((), ())), preferred_elem...  8.55 us
    all_gather x1, waiting for transfers between devices, per_device(): out_rows = lax.all_gather(out_weight, 'ctx', axis=1, tiled=True)  7.9 us
  transfers between devices with their start and end apart: 5, of which 5 were waited for; matrix products, arithmetic and copies ran while one was open for 7% of the time, Pallas kernels for 0%

commit v1 on v0

--- a/solution.py
+++ b/solution.py
@@ -49,10 +49,8 @@
 
 
 def per_device(tokens, qkv_weight, short_filter, long_filter, decay_rate, skip_gain, out_weight):
-    local_width = qkv_weight.shape[2]
     tap_count = long_filter.shape[1]
     span = short_filter.shape[1]
-    group_width = local_width // long_filter.shape[0]
     projected = jnp.einsum(
         "tr,src->sct",
         tokens,
@@ -64,25 +62,25 @@
     filters = (long_filter * jnp.exp(-decay_rate[:, None] * tap_index[None, :])).astype(
         jnp.bfloat16
     )
-    moved = lax.all_to_all(qkv, "ctx", split_axis=1, concat_axis=2, tiled=True)
-    share = moved.shape[1]
-    position = lax.axis_index("ctx")
-    part_short = lax.dynamic_slice_in_dim(short_filter, position * share, share, 2)
-    part_filters = lax.dynamic_slice_in_dim(
-        filters, position * (share // group_width), share // group_width, 0
+    halo = tap_count + span - 1
+    count = lax.axis_size("ctx")
+    tail = lax.ppermute(
+        qkv[:, :, qkv.shape[2] - halo :], "ctx", [(i, i + 1) for i in range(count - 1)]
     )
-    part_gain = lax.dynamic_slice_in_dim(skip_gain, position * share, share, 0)
-    leading = jnp.zeros((3, share, span - 1), jnp.bfloat16)
-    features = short_conv(jnp.concatenate([leading, moved], axis=2), part_short)
+    features = short_conv(jnp.concatenate([tail, qkv], axis=2), short_filter)
     gated = (features[1] * features[2]).astype(jnp.bfloat16)
-    previous = jnp.zeros((share, tap_count), jnp.bfloat16)
-    regrouped = long_mix(features, gated, previous, part_filters, part_gain)
-    mixed = lax.all_to_all(regrouped, "ctx", split_axis=1, concat_axis=0, tiled=True)
+    mixed = long_mix(
+        features[:, :, tap_count:],
+        gated[:, tap_count:],
+        gated[:, :tap_count],
+        filters,
+        skip_gain,
+    )
     out_rows = lax.all_gather(out_weight, "ctx", axis=1, tiled=True)
     summed = lax.psum_scatter(
         lax.dot_general(
             mixed, out_rows, (((0,), (0,)), ((), ())), preferred_element_type=jnp.float32
-        ),
+        ).astype(jnp.bfloat16),
         "tp",
         scatter_dimension=0,
         tiled=True,

time: 380 us -> 283 us (0.74)
  waiting for transfers between devices: 291 us -> 215 us
  local copies, waits for them, and re-layouts: 20.7 us -> 10.3 us
  starting transfers between devices: 13.5 us -> 3.39 us
    all_to_all x2 -> x0, waiting for transfers between devices: 81.3 us -> none  [the longest x1 66.1 us: per_device(): moved = lax.all_to_all(qkv, 'ctx', split_axis=1, concat_axis=2, tiled=True)]
    all_gather x1, waiting for transfers between devices: 7.9 us -> 38.4 us  [per_device(): out_rows = lax.all_gather(out_weight, 'ctx', axis=1, tiled=True)]
    reduce_scatter x1, waiting for transfers between devices: 74.5 us -> 48 us  [per_device(): lax.psum_scatter(lax.dot_general(mixed, out_rows, (((0,), (0,)), ((), ())...]
    all_to_all x2 -> x0, starting transfers between devices: 13.2 us -> none  [the longest x1 6.75 us: per_device(): moved = lax.all_to_all(qkv, 'ctx', split_axis=1, concat_axis=2, tiled=True)]
    all_to_all x2 -> x0, local copies, waits for them, and re-layouts: 6.15 us -> none  [per_device(): moved = lax.all_to_all(qkv, 'ctx', split_axis=1, concat_axis=2, tiled=True)]
    convert_element_type x2 -> x0, other arithmetic: 5.76 us -> none  [the longest x1 3.38 us: long_mix(): (features[0] * (filtered + gain[:, None] * gated.astype(jnp.float32))).as...]
    add x1, other arithmetic: 4.87 us -> 9.66 us  [short_conv(): result + short_filter[:, offset, :, None] * extended[:, :, start:start +...]
    reshape x2 -> x0, local copies, waits for them, and re-layouts: 4.1 us -> none  [the longest x1 2.59 us: long_mix(): filtered = current.reshape(channel_count, length)]
  transfers between devices with their start and end apart: 5 -> 4, of which waited for: 5 -> 4; matrix products, arithmetic and copies ran while one was open for 7% -> 13% of each run, Pallas kernels for 0% -> 0%
where the time goes in v1:
time: 283 us
  waiting for transfers between devices  215 us (76%)
  matrix products  30.6 us (11%)
  between operations  13.3 us (5%)
  other arithmetic  10.7 us (4%)
  local copies, waits for them, and re-layouts  10.3 us (4%)
  starting transfers between devices  3.39 us (1%)
    all_gather x1, waiting for transfers between devices, per_device(): lax.all_gather(qkv_weight, 'ctx', axis=1, tiled=True)  124 us
    reduce_scatter x1, waiting for transfers between devices, per_device(): lax.psum_scatter(lax.dot_general(mixed, out_rows, (((0,), (0,)), ((), ())...  48 us
    all_gather x1, waiting for transfers between devices, per_device(): out_rows = lax.all_gather(out_weight, 'ctx', axis=1, tiled=True)  38.4 us
    dot_general x1, matrix products, per_device(): jnp.einsum('tr,src->sct', tokens, lax.all_gather(qkv_weight, 'ctx', axis=...  14.8 us
    add x1, other arithmetic, short_conv(): result + short_filter[:, offset, :, None] * extended[:, :, start:start +...  9.66 us
    dot_general x1, matrix products, per_device(): lax.dot_general(mixed, out_rows, (((0,), (0,)), ((), ())), preferred_elem...  9.17 us
  transfers between devices with their start and end apart: 4, of which 4 were waited for; matrix products, arithmetic and copies ran while one was open for 13% of the time, Pallas kernels for 0%

profile of v1, /device:TPU:1, one launch (start us, length us, event | category | flops | bytes accessed | tf_op | source)
XLA Modules:
  0.0 282.9 jit_solution(6886937926897563706)
XLA Ops:
  6.5 1.9 copy.20
  8.5 0.0 all-gather.3.cloned.1.call-update
  8.5 0.0 all-gather.5.cloned.1.call-start
  8.5 0.7 all-gather.5.cloned.1.call-update
  9.2 0.0 reduce-scatter.2.cloned.1.call-start
  9.3 1.2 fusion.34
  10.5 0.7 neg.4
  11.2 0.0 copy-start.3
  11.3 124.4 %all-gather.3.cloned.1.call-done = bf16[3,4096,512]{1,2,0:T(8,128)(2,1)} async-done(((bf16[3,128,512]{1,2,0:T(8,128)(2,1)}), bf16[3,4096,512]{1,2,0:T(8,128)(2,1)}) %all-gather.3.cloned.1.call-update) | async-done | bytes 12582928 | tf_op jit(solution)/shard_map/all_gather | solution.py:57
  135.6 14.8 %fusion.10 = bf16[3,512,768]{2,1,0:T(8,128)(2,1)S(1)} fusion(bf16[3,4096,512]{1,2,0:T(8,128)(2,1)} %all-gather.3.cloned.1.call-done, bf16[768,4096]{1,0:T(8,128)(2,1)} %param.7), kind=kOutput, calls=%fused_computation.28 | convolution fusion | flops 9664856064 | bytes 21233664 | tf_op jit(solution)/shard_map/tr,src->sct/dot_general | solution.py:54
  150.4 0.3 slice.88
  150.8 1.0 copy.21
  151.8 3.3 %collective-permute-start = (bf16[3,512,134]{1,2,0:T(8,128)(2,1)}, bf16[3,512,134]{1,2,0:T(8,128)(2,1)}, u32[]{:S(2)}, u32[]{:S(2)}) collective-permute-start(bf16[3,512,134]{1,2,0:T(8,128)(2,1)} %copy.21), channel_id=1, source_target_pairs={{0,8},{8,16},{16,24},{24,32},{32,40},{40,48},{48,56},{56,64},{64,7... | collective-permute-start | bytes 1234952 | tf_op jit(solution)/shard_map/ppermute | solution.py:67
  155.1 3.5 %fusion.17 = (bf16[32,128,128,1]{2,0,1,3:T(8,128)(2,1)}, bf16[32,128,128,1]{2,0,1,3:T(8,128)(2,1)}) fusion(pred[128,128]{1,0:T(8,128)(4,1)S(1)} %iota_compare_fusion.2, s32[128,128]{1,0:T(8,128)S(1)} %add_select_fusion, f32[32,128]{1,0:T(8,128)S(1)} %copy-done.3, f32[32]{0:T(128)S(1)} %neg.4), kind=kOutput, calls=%fused_computation.37 | convolution fusion | flops 137375744 | bytes 2195584 | tf_op jit(solution)/shard_map/gk,kij->gij/dot_general | solution.py:23
  158.6 3.0 %collective-permute-done = bf16[3,512,134]{1,2,0:T(8,128)(2,1)} collective-permute-done((bf16[3,512,134]{1,2,0:T(8,128)(2,1)}, bf16[3,512,134]{1,2,0:T(8,128)(2,1)}, u32[]{:S(2)}, u32[]{:S(2)}) %collective-permute-start) | collective-permute-done | bytes 411680 | tf_op jit(solution)/shard_map/ppermute | solution.py:67
  161.6 1.3 copy.22
  162.9 9.7 %multiply_add_fusion = f32[3,512,896]{2,1,0:T(8,128)S(1)} fusion(bf16[3,512,768]{2,1,0:T(8,128)(2,1)S(1)} %fusion.10, bf16[3,512,134]{2,1,0:T(8,128)(2,1)S(1)} %copy.22, f32[3,512]{1,0:T(4,128)S(1)} %get-tuple-element.16, f32[3,512]{1,0:T(4,128)S(1)} %get-tuple-element.17, f32[3,512]{1,0:T(4,128)S(1)} %get-tuple-element.18, ...), kind=kLoop, calls=%fused_computation.11 | loop fusion | flops 56426496 | bytes 8318976 | tf_op jit(solution)/shard_map/add | solution.py:13
  172.6 2.4 copy-done
  175.0 0.2 fusion.13
  175.2 1.0 convert_element_type.62
  176.2 0.5 fusion.33
  176.7 0.0 slice-start
  176.7 2.2 fusion.19
  179.0 0.0 slice-start.1
  179.0 0.0 copy-start.2
  179.0 0.9 convolution_add_fusion
  179.9 0.6 copy.27
  180.5 0.2 fusion.39
  180.7 38.4 %all-gather.5.cloned.1.call-done = bf16[512,4096]{1,0:T(8,128)(2,1)} async-done(((bf16[512,128]{1,0:T(8,128)(2,1)}), bf16[512,4096]{1,0:T(8,128)(2,1)}) %all-gather.5.cloned.1.call-update) | async-done | bytes 4194320 | tf_op jit(solution)/shard_map/all_gather | solution.py:79
  219.2 9.2 %convolution_convert_fusion = bf16[768,4096]{1,0:T(8,128)(2,1)} fusion(bf16[512,4096]{1,0:T(8,128)(2,1)} %all-gather.5.cloned.1.call-done, f32[64,8,6,128]{3,2,1,0:T(8,128)S(1)} %bitcast.49, f32[3,512,896]{2,1,0:T(8,128)} %copy-done, bf16[512,896]{1,0:T(8,128)(2,1)S(1)} %fusion.39, f32[512]{0:T(512)S(1)} %copy-done.2), kind=kOutput, calls=%fused_computation.8 | convolution fusion | flops 3226337280 | bytes 14944256 | tf_op jit(solution)/shard_map/dot_general | solution.py:81
  228.3 0.0 reduce-scatter.2.cloned.1.call-update
  228.4 48.0 %reduce-scatter.2.cloned.1.call-done = bf16[96,4096]{1,0:T(8,128)(2,1)} async-done(((bf16[768,4096]{1,0:T(8,128)(2,1)}), bf16[96,4096]{1,0:T(8,128)(2,1)}) %reduce-scatter.2.cloned.1.call-update) | async-done | bytes 786448 | tf_op jit(solution)/shard_map/reduce_scatter | solution.py:80
  (15 shorter events, 0.1 us)
Async XLA Ops:
  6.5 129.1 %all-gather.3.cloned.1.call-start = ((), (), s32[]{:S(2)}) async-start(), calls=%async_computation.1 | async-start | bytes 12976128 | tf_op jit(solution)/shard_map/all_gather | solution.py:57
  8.5 210.7 %all-gather.5.cloned.1.call-start = ((), (), s32[]{:S(2)}) async-start(), calls=%async_computation.2 | async-start | bytes 4325376 | tf_op jit(solution)/shard_map/all_gather | solution.py:79
  9.2 267.2 %reduce-scatter.2.cloned.1.call-start = ((), (), s32[]{:S(2)}) async-start(), calls=%async_computation.3 | async-start | bytes 7077888 | tf_op jit(solution)/shard_map/reduce_scatter | solution.py:80
  11.2 143.8 %copy-start.3 = (f32[32,128]{1,0:T(8,128)S(1)}, f32[32,128]{1,0:T(8,128)}, u32[]{:S(2)}) copy-start(f32[32,128]{1,0:T(8,128)} %param.10) | copy-start | bytes 49156
  151.8 9.9 %collective-permute-start = (bf16[3,512,134]{1,2,0:T(8,128)(2,1)}, bf16[3,512,134]{1,2,0:T(8,128)(2,1)}, u32[]{:S(2)}, u32[]{:S(2)}) collective-permute-start(bf16[3,512,134]{1,2,0:T(8,128)(2,1)} %copy.21), channel_id=1, source_target_pairs={{0,8},{8,16},{16,24},{24,32},{32,40},{40,48},{48,56},{56,64},{64,7... | collective-permute-start | bytes 1234952 | tf_op jit(solution)/shard_map/ppermute | solution.py:67
  172.6 2.4 copy-start
  175.2 3.8 %copy-start.1 = (bf16[32,128,128,1]{2,0,1,3:T(8,128)(2,1)S(1)}, bf16[32,128,128,1]{2,0,1,3:T(8,128)(2,1)}, u32[]{:S(2)}) copy-start(bf16[32,128,128,1]{2,0,1,3:T(8,128)(2,1)} %get-tuple-element.5) | copy-start | bytes 3145732
  176.7 3.8 %slice-start = ((s8[5505024]{0:T(1024)(128)(4,1)}), s8[4194304]{0:T(1024)(128)(4,1)S(1)}, s32[]{:S(2)}) async-start(s8[5505024]{0:T(1024)(128)(4,1)} %bitcast.47), calls=%async_computation.4 | async-start | bytes 8388608
  179.0 1.6 slice-start.1
  179.0 40.2 %copy-start.2 = (f32[512]{0:T(512)S(1)}, f32[512]{0:T(512)}, u32[]{:S(2)}) copy-start(f32[512]{0:T(512)} %param.12) | copy-start | bytes 6148
Sparse Core Ops, SparseCore 0:
  9.8 125.8 all-gather.2
  138.1 81.0 all-gather.4
  228.5 47.8 reduce-scatter.1

commit v2 on v1

v2 whole, which is shorter than its diff:
```python
import jax
import jax.numpy as jnp
from jax import lax
from jax.experimental import pallas as pl
from jax.experimental.pallas import tpu as pltpu
from jax.sharding import PartitionSpec as P

MESH = pl.DeviceIdType.MESH
NZ, NX, NY = 8, 4, 4
ROUNDS = (0, 1, 7, 2, 6, 3, 5, 4)
CHUNKS = ((0, (0,)), (1, (1, 7)), (7, ()), (2, (2, 6)), (6, ()), (3, (3, 5)), (5, ()), (4, (4,)))


class Gather:
    def __init__(self, place, slot, send_sem, recv_sem):
        self.z, self.x, self.step = place
        self.slot, self.send_sem, self.recv_sem = slot, send_sem, recv_sem
        self.sent = []

    def source(self, dz, dx):
        z = lax.rem(self.z - self.step * dz + NZ, NZ)
        x = lax.rem(self.x - self.step * dx + NX, NX)
        return z * NX + x

    def copy(self, part, dz, dx, axis, way):
        ref = self.slot(part, self.source(dz, dx))
        z, x = self.z, self.x
        if axis == "z":
            z, dz = lax.rem(z + way * self.step + NZ, NZ), (dz + way) % NZ
        else:
            x, dx = lax.rem(x + way * self.step + NX, NX), (dx + way) % NX
        return pltpu.make_async_remote_copy(
            src_ref=ref,
            dst_ref=ref,
            send_sem=self.send_sem.at[part, dz, dx],
            recv_sem=self.recv_sem.at[part, dz, dx],
            device_id={"ctx": z * NX + x},
            device_id_type=MESH,
        )

    def send(self, *args):
        copy = self.copy(*args)
        copy.start()
        self.sent.append(copy)

    def wait(self, part, dz, dx):
        if (dz, dx) != (0, 0):
            ref = self.slot(part, self.source(dz, dx))
            pltpu.make_async_remote_copy(
                src_ref=ref,
                dst_ref=ref,
                send_sem=self.send_sem.at[part, dz, dx],
                recv_sem=self.recv_sem.at[part, dz, dx],
                device_id={"ctx": lax.rem(self.z + 1, NZ) * NX + self.x},
                device_id_type=MESH,
            ).wait_recv()

    def along_z(self, part, dz, dx):
        if dz <= NZ // 2 - 1:
            self.send(part, dz, dx, "z", 1)
        if dz == 0 or dz > NZ // 2 + 1:
            self.send(part, dz, dx, "z", -1)

    def along_x(self, part, dz, dx):
        if dx <= NX // 2 - 1:
            self.send(part, dz, dx, "x", 1)
        if dx == 0 or dx > NX // 2 + 1:
            self.send(part, dz, dx, "x", -1)

    def arrive0(self, dz, dx):
        self.wait(0, dz, dx)
        if dx == 0:
            self.along_z(0, dz, dx)
        self.along_x(0, dz, dx)

    def arrive1(self, dz, dx):
        self.wait(1, dz, dx)
        if dz == 0:
            self.along_x(1, dz, dx)
        self.along_z(1, dz, dx)

    def service(self, index):
        dz = ROUNDS[index]
        self.arrive0(dz, 0)
        for dx in (0, 1, 3, 2):
            self.arrive1(dz, dx)
        self.arrive0(dz, 1)

    def complete(self, dz):
        self.arrive0(dz, 3)
        self.arrive0(dz, 2)

    def finish(self):
        for copy in self.sent:
            copy.wait_send()


def kernel(
    tokens_hbm, qkv_hbm, short_ref, long_ref, decay_ref, gain_ref, out_hbm,
    result_ref,
    tok, wq, wo, acc, quer, gat, band, mix, mixp, own,
    cs_send, cs_recv, fs, fr, ms, mr, js, jr, tail_send, tail_recv, halo,
    local_sem, wq_ss, wq_rs, wo_ss, wo_rs, cs_ss, cs_rs, y_ss, y_rs, halo_ss, halo_rs,
):
    ctx, tp = lax.axis_index("ctx"), lax.axis_index("tp")
    z, x = lax.div(ctx, NX), lax.rem(ctx, NX)
    y, core = lax.div(tp, 2), lax.rem(tp, 2)
    step = 1 - 2 * core
    tcount, depth = tok.shape
    share = qkv_hbm.shape[1]
    width = qkv_hbm.shape[2]
    count = NZ * NX
    block = tcount // (2 * NY)
    half = NY * block

    local = [pltpu.make_async_copy(qkv_hbm.at[i], wq.at[pl.ds(pl.multiple_of(ctx * share, share), share), pl.ds(i * width, width)], local_sem.at[i]) for i in range(3)]
    local.append(pltpu.make_async_copy(out_hbm, wo.at[ctx], local_sem.at[3]))
    local.append(pltpu.make_async_copy(tokens_hbm, tok, local_sem.at[4]))
    for copy in local:
        copy.start()

    after = {"ctx": lax.rem(ctx + 1, count)}
    partner = {"tp": tp + step}
    y_up = {"tp": lax.rem(y + step + NY, NY) * 2 + core}
    y_down = {"tp": lax.rem(y - step + NY, NY) * 2 + core}
    barrier = pltpu.get_barrier_semaphore()
    neighbours = [
        {"ctx": lax.rem(z + 1, NZ) * NX + x},
        {"ctx": lax.rem(z + NZ - 1, NZ) * NX + x},
        {"ctx": z * NX + lax.rem(x + 1, NX)},
        {"ctx": z * NX + lax.rem(x + NX - 1, NX)},
        after,
        {"ctx": lax.rem(ctx + count - 1, count)},
        partner,
        y_up,
        y_down,
    ]
    for device in neighbours:
        pl.semaphore_signal(barrier, inc=1, device_id=device, device_id_type=MESH)
    pl.semaphore_wait(barrier, len(neighbours))

    cut = 7 * 128
    ocut = 304

    def wq_slot(part, source):
        rows = pl.ds(pl.multiple_of(source * share, share), share)
        return wq.at[rows, pl.ds(0, cut)] if part == 0 else wq.at[rows, pl.ds(cut, 3 * width - cut)]

    def wo_slot(part, source):
        return wo.at[source, pl.ds(0, ocut), :] if part == 0 else wo.at[source, pl.ds(ocut, width - ocut), :]

    place = (z, x, step)
    wg = Gather(place, wq_slot, wq_ss, wq_rs)
    og = Gather(place, wo_slot, wo_ss, wo_rs)

    for copy in local[:3]:
        copy.wait()
    wg.service(0)
    for copy in local[3:]:
        copy.wait()

    taps = long_ref.shape[1]
    lane = lax.broadcasted_iota(jnp.int32, (1, taps), 1).astype(jnp.float32)
    row_id = lax.broadcasted_iota(jnp.int32, (taps, taps), 0)
    col_id = lax.broadcasted_iota(jnp.int32, (taps, taps), 1)

    def build(group, carry):
        filt = long_ref[pl.ds(group, 1), :] * jnp.exp(-decay_ref[pl.ds(group, 1), :] * lane)
        ring = pltpu.roll(jnp.broadcast_to(filt, (taps, taps)), 0, 1, stride=1, stride_axis=0).T
        rows = pl.ds(pl.multiple_of(group * taps, taps), taps)
        band[rows, 0:taps] = jnp.where(col_id > row_id, ring, 0.0).astype(jnp.bfloat16)
        band[rows, taps : 2 * taps] = jnp.where(col_id <= row_id, ring, 0.0).astype(jnp.bfloat16)
        return carry

    lax.fori_loop(0, long_ref.shape[0], build, 0)

    lead = 8
    span = NX * share
    tile = 256

    def project(dz, first, last):
        source = lax.rem(z - step * dz + NZ, NZ)
        rows = pl.ds(pl.multiple_of(source * span, span), span)

        def one(n, carry):
            cols = pl.ds(pl.multiple_of(n * tile, tile), tile)
            part = jnp.dot(tok[:, rows], wq[rows, cols], preferred_element_type=jnp.float32)
            if not first:
                part = part + acc[lead:, cols]
            if last:
                part = part.astype(jnp.bfloat16).astype(jnp.float32)
            acc[lead:, cols] = part
            return carry

        lax.fori_loop(0, 3 * width // tile, one, 0)

    for index in range(1, NZ):
        wg.service(index)
        dz = ROUNDS[index - 1]
        wg.complete(dz)
        project(dz, index == 1, False)
    og.service(0)
    wg.complete(ROUNDS[-1])
    project(ROUNDS[-1], False, True)

    def remote(src, dst, ss, rs, device):
        return pltpu.make_async_remote_copy(src_ref=src, dst_ref=dst, send_sem=ss, recv_sem=rs, device_id=device, device_id_type=MESH)

    tail_send[...] = acc[lead + tcount - 16 :, :].astype(jnp.bfloat16)
    tail_copy = remote(tail_send, tail_recv, halo_ss.at[0], halo_rs.at[0], after)
    tail_copy.start()

    reach = short_ref.shape[1]
    lanes = 128

    def feature(s, r, c):
        cols = pl.ds(pl.multiple_of(s * width + c * lanes, lanes), lanes)
        own_cols = pl.ds(pl.multiple_of(c * lanes, lanes), lanes)
        window = acc[pl.ds(pl.multiple_of(r * taps, taps), taps + lead), cols]
        total = window[lead:] * short_ref[s, 0:1, own_cols]
        for j in range(1, reach):
            total = total + pltpu.roll(window, j, 0)[lead:] * short_ref[s, j : j + 1, own_cols]
        return total

    def features(r, c):
        rows = pl.ds(pl.multiple_of(r * taps, taps), taps)
        cols = pl.ds(pl.multiple_of(c * lanes, lanes), lanes)
        gat[pl.ds(pl.multiple_of(r * taps + taps, taps), taps), cols] = (feature(1, r, c) * feature(2, r, c)).astype(jnp.bfloat16)
        quer[rows, cols] = feature(0, r, c)

    tiles = width // lanes
    blocks = tcount // taps
    lax.fori_loop(0, tiles, lambda c, k: (features(blocks - 1, c), k)[1], 0)
    halo_copy = remote(gat.at[pl.ds(tcount, taps), :], halo, halo_ss.at[1], halo_rs.at[1], after)
    halo_copy.start()
    og.service(1)

    def later(i, carry):
        features(lax.div(i, tiles) + 1, lax.rem(i, tiles))
        return carry

    lax.fori_loop(0, (blocks - 2) * tiles, later, 0)
    tail_copy.wait_recv()
    acc[0:lead, :] = jnp.where(ctx > 0, tail_recv[...].astype(jnp.float32)[16 - lead :, :], 0.0)
    lax.fori_loop(0, tiles, lambda c, k: (features(0, c), k)[1], 0)
    og.service(2)
    og.complete(0)
    halo_copy.wait_recv()
    gat[0:taps, :] = jnp.where(ctx > 0, halo[...].astype(jnp.float32), 0.0).astype(jnp.bfloat16)

    group_of = lax.broadcasted_iota(jnp.int32, (taps, 2 * lanes), 1) % lanes // 16
    per_tile = lanes // 16

    def convolve(i, carry):
        p, c = lax.div(i, tiles), lax.rem(i, tiles)
        cols = pl.ds(pl.multiple_of(c * lanes, lanes), lanes)
        base = p * 2 * taps

        def at(offset, size):
            return pl.ds(pl.multiple_of(base + offset, taps), size)

        right = jnp.concatenate([gat[at(0, 2 * taps), cols], gat[at(taps, 2 * taps), cols]], axis=1)
        left = band[pl.ds(pl.multiple_of(c * per_tile * taps, taps), per_tile * taps), :]
        every = jnp.dot(left, right, preferred_element_type=jnp.float32)
        total = every[0:taps]
        for g in range(1, per_tile):
            total = jnp.where(group_of >= g, every[g * taps : (g + 1) * taps], total)
        gain = gain_ref[0:1, cols]
        for h in range(2):
            gated = gat[at((h + 1) * taps, taps), cols].astype(jnp.float32)
            rows = at(h * taps, taps)
            mix[rows, cols] = (quer[rows, cols] * (total[:, h * lanes : (h + 1) * lanes] + gain * gated)).astype(jnp.bfloat16)
        return carry

    pairs = blocks // 2
    lax.fori_loop(0, tiles, convolve, 0)
    og.service(3)
    og.complete(ROUNDS[1])
    og.complete(ROUNDS[2])
    lax.fori_loop(tiles, pairs * tiles, convolve, 0)

    for side in range(2):
        ahead = -step if side == 0 else step
        to_core = 1 - core if side == 0 else core
        for j in range(NY):
            to = lax.rem(y + ahead * j + NY, NY) * 2 + to_core
            mixp[side * half + j * block : side * half + (j + 1) * block, :] = mix[pl.ds(pl.multiple_of(to * block, 16), block), :]

    def stage0(k):
        offset, needs = CHUNKS[k]
        zsrc = lax.rem(z + offset, NZ)
        for i in range(NX // 2):
            right = jnp.concatenate([wo[zsrc * NX + 2 * i], wo[zsrc * NX + 2 * i + 1]], axis=1)
            cols = slice(2 * i * share, 2 * (i + 1) * share)
            cs_send[k, :, cols] = jnp.dot(mixp[0:half, :], right, preferred_element_type=jnp.float32).astype(jnp.bfloat16)
        copy = remote(cs_send.at[k], cs_recv.at[k], cs_ss.at[k], cs_rs.at[k], partner)
        copy.start()
        for i in range(NX // 2):
            right = jnp.concatenate([wo[zsrc * NX + 2 * i], wo[zsrc * NX + 2 * i + 1]], axis=1)
            cols = slice(2 * i * share, 2 * (i + 1) * share)
            own[k % 4, :, cols] = jnp.dot(mixp[half:, :], right, preferred_element_type=jnp.float32)
        return copy

    def rows_of(j):
        return slice(j * block, (j + 1) * block)

    def stage1(k):
        cs[k].wait_recv()
        slot = k % 4
        fs[k] = (own[slot, rows_of(2)] + cs_recv[k, rows_of(2)].astype(jnp.float32)).astype(jnp.bfloat16)
        first = remote(fs.at[k], fr.at[k], y_ss.at[0, k], y_rs.at[0, k], y_up)
        first.start()
        ms[k] = (own[slot, rows_of(3)] + cs_recv[k, rows_of(3)].astype(jnp.float32)).astype(jnp.bfloat16)
        minor = remote(ms.at[k], mr.at[k], y_ss.at[1, k], y_rs.at[1, k], y_down)
        minor.start()
        own[slot, 0 : 2 * block] = own[slot, 0 : 2 * block] + cs_recv[k, 0 : 2 * block].astype(jnp.float32)
        return first, minor

    def stage2(k):
        ys[k][0].wait_recv()
        js[k] = (own[k % 4, rows_of(1)] + fr[k].astype(jnp.float32)).astype(jnp.bfloat16)
        joined = remote(js.at[k], jr.at[k], y_ss.at[2, k], y_rs.at[2, k], y_up)
        joined.start()
        return joined

    def stage3(k):
        ys[k][1].wait_recv()
        jn[k].wait_recv()
        zsrc = lax.rem(z + CHUNKS[k][0], NZ)
        total = own[k % 4, rows_of(0)] + mr[k].astype(jnp.float32) + jr[k].astype(jnp.float32)
        result_ref[:, pl.ds(pl.multiple_of(zsrc * span, span), span)] = total.astype(jnp.bfloat16)

    cs, ys, jn = {}, {}, {}
    done = {0, ROUNDS[1], ROUNDS[2]}
    served = 3
    for k in range(NZ + 3):
        if k < NZ:
            for dz in CHUNKS[k][1]:
                while dz not in done:
                    if served < NZ - 1:
                        served += 1
                        og.service(served)
                    if dz == ROUNDS[served] or dz in ROUNDS[:served]:
                        og.complete(dz)
                        done.add(dz)
            cs[k] = stage0(k)
        if 1 <= k < NZ + 1:
            ys[k - 1] = stage1(k - 1)
        if 2 <= k < NZ + 2:
            jn[k - 2] = stage2(k - 2)
        if k >= 3:
            stage3(k - 3)

    wg.finish()
    og.finish()
    tail_copy.wait_send()
    halo_copy.wait_send()
    for k in range(NZ):
        cs[k].wait_send()
        ys[k][0].wait_send()
        ys[k][1].wait_send()
        jn[k].wait_send()


def per_device(tokens, qkv_weight, short_filter, long_filter, decay_rate, skip_gain, out_weight):
    tcount, depth = tokens.shape
    _, share, width = qkv_weight.shape
    taps = long_filter.shape[1]
    groups = long_filter.shape[0]
    span = NX * share
    block = tcount // (2 * NY)
    half = NY * block
    bf, f32 = jnp.bfloat16, jnp.float32
    dma = pltpu.SemaphoreType.DMA
    any_spec = pl.BlockSpec(memory_space=pl.ANY)
    vmem = pl.BlockSpec(memory_space=pltpu.VMEM)
    small = (NZ, block, span)
    return pl.pallas_call(
        kernel,
        out_shape=jax.ShapeDtypeStruct((block, depth), bf),
        in_specs=[any_spec, any_spec, vmem, vmem, vmem, vmem, any_spec],
        out_specs=vmem,
        scratch_shapes=[
            pltpu.VMEM((tcount, depth), bf),
            pltpu.VMEM((depth, 3 * width), bf),
            pltpu.VMEM((NZ * NX, width, share), bf),
            pltpu.VMEM((8 + tcount, 3 * width), f32),
            pltpu.VMEM((tcount, width), f32),
            pltpu.VMEM((taps + tcount, width), bf),
            pltpu.VMEM((groups * taps, 2 * taps), bf),
            pltpu.VMEM((tcount, width), bf),
            pltpu.VMEM((tcount, width), bf),
            pltpu.VMEM((4, half, span), f32),
            pltpu.VMEM((NZ, half, span), bf),
            pltpu.VMEM((NZ, half, span), bf),
            *[pltpu.VMEM(small, bf) for _ in range(6)],
            pltpu.VMEM((16, 3 * width), bf),
            pltpu.VMEM((16, 3 * width), bf),
            pltpu.VMEM((taps, width), bf),
            dma((5,)),
            dma((2, NZ, NX)),
            dma((2, NZ, NX)),
            dma((2, NZ, NX)),
            dma((2, NZ, NX)),
            dma((NZ,)),
            dma((NZ,)),
            dma((3, NZ)),
            dma((3, NZ)),
            dma((2,)),
            dma((2,)),
        ],
        compiler_params=pltpu.CompilerParams(
            collective_id=0, has_side_effects=True, vmem_limit_bytes=67043328
        ),
    )(
        tokens,
        qkv_weight,
        short_filter,
        long_filter,
        decay_rate[:, None],
        skip_gain[None, :],
        out_weight,
    )


def solution(mesh):
    in_specs = (
        P("ctx", None),
        P(None, "ctx", "tp"),
        P(None, None, "tp"),
        P("tp", None),
        P("tp"),
        P("tp"),
        P("tp", "ctx"),
    )
    out_specs = P(("ctx", "tp"), None)
    return jax.shard_map(
        per_device, mesh=mesh, in_specs=in_specs, out_specs=out_specs, check_vma=False
    )
```

time: 283 us -> 185 us (0.65)
  the two profiles are of different devices: /device:TPU:1 before, /device:TPU:2 now
where the time goes in v2:
time: 185 us; the launch traced here: 184 us
  Pallas kernels  181 us (98%)
  local copies, waits for them, and re-layouts  3.4 us (2%)
    pallas_call x1, Pallas kernels, per_device(): pl.pallas_call(kernel, out_shape=jax.ShapeDtypeStruct((block, depth), bf)...  181 us

profile of v2, /device:TPU:2, one launch (start us, length us, event | category | flops | bytes accessed | tf_op | source)
XLA Modules:
  0.0 184.4 jit_solution(13880400543971191700)
XLA Ops:
  0.0 1.3 copy.8.decay_ref
  1.3 181.0 %shard_map.73 = bf16[96,4096]{1,0:T(8,128)(2,1)} custom-call(bf16[768,4096]{1,0:T(8,128)(2,1)} %tokens_hbm.1, bf16[3,128,512]{2,1,0:T(8,128)(2,1)} %qkv_hbm.1, f32[3,7,512]{2,1,0:T(8,128)} %short_ref.1, f32[32,128]{1,0:T(8,128)} %long_ref.1, f32[32,1]{1,0:T(8,128)} %copy.8.decay_ref, f32[1,512]{1,0:T(1,128)} %bitcast.2, bf16[512,128]{1,0:T(8,128)(2,1)} %out_hbm.1), custom_call_target="tpu_custom_call" | custom-call | tf_op jit(solution)/shard_map/pallas_call | solution.py:378
  182.4 2.1 %copy.10 = bf16[96,4096]{1,0:T(8,128)(2,1)} copy(bf16[96,4096]{1,0:T(8,128)(2,1)} %shard_map.73) | data formatting | bytes 1572864

commit v3 on v2

--- a/solution.py
+++ b/solution.py
@@ -7,8 +7,15 @@
 
 MESH = pl.DeviceIdType.MESH
 NZ, NX, NY = 8, 4, 4
-ROUNDS = (0, 1, 7, 2, 6, 3, 5, 4)
-CHUNKS = ((0, (0,)), (1, (1, 7)), (7, ()), (2, (2, 6)), (6, ()), (3, (3, 5)), (5, ()), (4, (4,)))
+ORDER = (
+    36, 60, 1, 3, 4, 28, 33, 35, 2, 40, 56, 5, 7, 8, 24, 37, 61, 29, 31, 39, 63, 34, 11, 44, 52,
+    6, 27, 12, 20, 9, 25, 41, 57, 43, 59, 15, 30, 38, 62, 13, 23, 48, 53, 21, 10, 55, 16, 26,
+    58, 45, 14, 47, 19, 42, 22, 54, 49, 17, 64, 51, 46, 124, 100, 67, 92, 99, 68, 18, 65, 120,
+    50, 97, 104, 88, 93, 95, 103, 127, 69, 71, 72, 116, 66, 101, 125, 98, 108, 91, 89, 84, 107,
+    75, 123, 94, 76, 70, 121, 105, 73, 126, 102, 87, 90, 119, 112, 117, 111, 79, 85, 77, 122,
+    80, 74, 109, 106, 115, 86, 118, 78, 113, 83, 110, 81, 114, 82,
+)
+CHUNKS = ((0, (0,)), (1, (1, 7)), (7, (1, 7)), (2, (2, 6)), (6, (2, 6)), (3, (3, 5)), (5, (3, 5)), (4, (4,)))
 
 
 class Gather:
@@ -55,40 +62,25 @@
                 device_id_type=MESH,
             ).wait_recv()
 
-    def along_z(self, part, dz, dx):
-        if dz <= NZ // 2 - 1:
-            self.send(part, dz, dx, "z", 1)
-        if dz == 0 or dz > NZ // 2 + 1:
-            self.send(part, dz, dx, "z", -1)
-
-    def along_x(self, part, dz, dx):
-        if dx <= NX // 2 - 1:
-            self.send(part, dz, dx, "x", 1)
-        if dx == 0 or dx > NX // 2 + 1:
-            self.send(part, dz, dx, "x", -1)
-
-    def arrive0(self, dz, dx):
-        self.wait(0, dz, dx)
-        if dx == 0:
-            self.along_z(0, dz, dx)
-        self.along_x(0, dz, dx)
-
-    def arrive1(self, dz, dx):
-        self.wait(1, dz, dx)
-        if dz == 0:
-            self.along_x(1, dz, dx)
-        self.along_z(1, dz, dx)
-
-    def service(self, index):
-        dz = ROUNDS[index]
-        self.arrive0(dz, 0)
-        for dx in (0, 1, 3, 2):
-            self.arrive1(dz, dx)
-        self.arrive0(dz, 1)
-
-    def complete(self, dz):
-        self.arrive0(dz, 3)
-        self.arrive0(dz, 2)
+    def targets(self, part, dz, dx):
+        along_z = [w for w, go in ((1, dz < NZ // 2), (-1, dz == 0 or dz > NZ // 2 + 1)) if go]
+        along_x = [w for w, go in ((1, dx < NX // 2), (-1, dx == 0 or dx > NX // 2 + 1)) if go]
+        if part == 0:
+            first = [(part, dz, dx, "x", w) for w in along_x]
+            return first, [(part, dz, dx, "z", w) for w in along_z] if dx == 0 else []
+        first = [(part, dz, dx, "z", w) for w in along_z]
+        return first, [(part, dz, dx, "x", w) for w in along_x] if dz == 0 else []
+
+    def begin(self):
+        both = [self.targets(part, 0, 0) for part in range(2)]
+        for target in [t for i in range(2) for pair in both for t in pair[i]]:
+            self.send(*target)
+
+    def arrive(self, part, dz, dx):
+        self.wait(part, dz, dx)
+        first, second = self.targets(part, dz, dx)
+        for target in first + second:
+            self.send(*target)
 
     def finish(self):
         for copy in self.sent:
@@ -155,7 +147,7 @@
 
     for copy in local[:3]:
         copy.wait()
-    wg.service(0)
+    wg.begin()
     for copy in local[3:]:
         copy.wait()
 
@@ -178,12 +170,13 @@
     span = NX * share
     tile = 256
 
-    def project(dz, first, last):
+    def project(dz, first, last, part_of):
         source = lax.rem(z - step * dz + NZ, NZ)
         rows = pl.ds(pl.multiple_of(source * span, span), span)
+        loops = 3 * width // tile // 2
 
         def one(n, carry):
-            cols = pl.ds(pl.multiple_of(n * tile, tile), tile)
+            cols = pl.ds(pl.multiple_of((part_of * loops + n) * tile, tile), tile)
             part = jnp.dot(tok[:, rows], wq[rows, cols], preferred_element_type=jnp.float32)
             if not first:
                 part = part + acc[lead:, cols]
@@ -192,23 +185,17 @@
             acc[lead:, cols] = part
             return carry
 
-        lax.fori_loop(0, 3 * width // tile, one, 0)
-
-    for index in range(1, NZ):
-        wg.service(index)
-        dz = ROUNDS[index - 1]
-        wg.complete(dz)
-        project(dz, index == 1, False)
-    og.service(0)
-    wg.complete(ROUNDS[-1])
-    project(ROUNDS[-1], False, True)
+        lax.fori_loop(0, loops, one, 0)
 
     def remote(src, dst, ss, rs, device):
         return pltpu.make_async_remote_copy(src_ref=src, dst_ref=dst, send_sem=ss, recv_sem=rs, device_id=device, device_id_type=MESH)
 
-    tail_send[...] = acc[lead + tcount - 16 :, :].astype(jnp.bfloat16)
-    tail_copy = remote(tail_send, tail_recv, halo_ss.at[0], halo_rs.at[0], after)
-    tail_copy.start()
+    flight = {}
+
+    def send_tail():
+        tail_send[...] = acc[lead + tcount - 16 :, :].astype(jnp.bfloat16)
+        flight["tail"] = remote(tail_send, tail_recv, halo_ss.at[0], halo_rs.at[0], after)
+        flight["tail"].start()
 
     reach = short_ref.shape[1]
     lanes = 128
@@ -230,23 +217,21 @@
 
     tiles = width // lanes
     blocks = tcount // taps
-    lax.fori_loop(0, tiles, lambda c, k: (features(blocks - 1, c), k)[1], 0)
-    halo_copy = remote(gat.at[pl.ds(tcount, taps), :], halo, halo_ss.at[1], halo_rs.at[1], after)
-    halo_copy.start()
-    og.service(1)
-
-    def later(i, carry):
-        features(lax.div(i, tiles) + 1, lax.rem(i, tiles))
-        return carry
-
-    lax.fori_loop(0, (blocks - 2) * tiles, later, 0)
-    tail_copy.wait_recv()
-    acc[0:lead, :] = jnp.where(ctx > 0, tail_recv[...].astype(jnp.float32)[16 - lead :, :], 0.0)
-    lax.fori_loop(0, tiles, lambda c, k: (features(0, c), k)[1], 0)
-    og.service(2)
-    og.complete(0)
-    halo_copy.wait_recv()
-    gat[0:taps, :] = jnp.where(ctx > 0, halo[...].astype(jnp.float32), 0.0).astype(jnp.bfloat16)
+
+    def feature_rows(r):
+        lax.fori_loop(0, tiles, lambda c, k: (features(r, c), k)[1], 0)
+
+    def send_halo():
+        flight["halo"] = remote(gat.at[pl.ds(tcount, taps), :], halo, halo_ss.at[1], halo_rs.at[1], after)
+        flight["halo"].start()
+
+    def take_tail():
+        flight["tail"].wait_recv()
+        acc[0:lead, :] = jnp.where(ctx > 0, tail_recv[...].astype(jnp.float32)[16 - lead :, :], 0.0)
+
+    def take_halo():
+        flight["halo"].wait_recv()
+        gat[0:taps, :] = jnp.where(ctx > 0, halo[...].astype(jnp.float32), 0.0).astype(jnp.bfloat16)
 
     group_of = lax.broadcasted_iota(jnp.int32, (taps, 2 * lanes), 1) % lanes // 16
     per_tile = lanes // 16
@@ -272,19 +257,13 @@
             mix[rows, cols] = (quer[rows, cols] * (total[:, h * lanes : (h + 1) * lanes] + gain * gated)).astype(jnp.bfloat16)
         return carry
 
-    pairs = blocks // 2
-    lax.fori_loop(0, tiles, convolve, 0)
-    og.service(3)
-    og.complete(ROUNDS[1])
-    og.complete(ROUNDS[2])
-    lax.fori_loop(tiles, pairs * tiles, convolve, 0)
-
-    for side in range(2):
-        ahead = -step if side == 0 else step
-        to_core = 1 - core if side == 0 else core
-        for j in range(NY):
-            to = lax.rem(y + ahead * j + NY, NY) * 2 + to_core
-            mixp[side * half + j * block : side * half + (j + 1) * block, :] = mix[pl.ds(pl.multiple_of(to * block, 16), block), :]
+    def order_rows():
+        for side in range(2):
+            ahead = -step if side == 0 else step
+            to_core = 1 - core if side == 0 else core
+            for j in range(NY):
+                to = lax.rem(y + ahead * j + NY, NY) * 2 + to_core
+                mixp[side * half + j * block : side * half + (j + 1) * block, :] = mix[pl.ds(pl.multiple_of(to * block, 16), block), :]
 
     def stage0(k):
         offset, needs = CHUNKS[k]
@@ -331,18 +310,9 @@
         result_ref[:, pl.ds(pl.multiple_of(zsrc * span, span), span)] = total.astype(jnp.bfloat16)
 
     cs, ys, jn = {}, {}, {}
-    done = {0, ROUNDS[1], ROUNDS[2]}
-    served = 3
-    for k in range(NZ + 3):
+
+    def stages(k):
         if k < NZ:
-            for dz in CHUNKS[k][1]:
-                while dz not in done:
-                    if served < NZ - 1:
-                        served += 1
-                        og.service(served)
-                    if dz == ROUNDS[served] or dz in ROUNDS[:served]:
-                        og.complete(dz)
-                        done.add(dz)
             cs[k] = stage0(k)
         if 1 <= k < NZ + 1:
             ys[k - 1] = stage1(k - 1)
@@ -351,10 +321,54 @@
         if k >= 3:
             stage3(k - 3)
 
+    def mixing():
+        pairs = blocks // 2
+        yield send_tail
+        yield lambda: (feature_rows(blocks - 1), send_halo())
+        for r in range(blocks - 2, 0, -1):
+            yield lambda r=r: feature_rows(r)
+        yield lambda: (take_tail(), feature_rows(0))
+        for p in range(pairs - 1, -1, -1):
+            if p == 0:
+                yield take_halo
+            yield lambda p=p: lax.fori_loop(p * tiles, p * tiles + tiles // 2, convolve, 0)
+            yield lambda p=p: lax.fori_loop(p * tiles + tiles // 2, (p + 1) * tiles, convolve, 0)
+        yield order_rows
+
+    queue, seen, projected, chunk = [], {(p, 0, 0) for p in range(4)}, 0, 0
+    ready = set()
+    for code in ORDER:
+        part, dz, dx = code // 32, code % 32 // 4, code % 4
+        if code == 64:
+            og.begin()
+            continue
+        (wg if part < 2 else og).arrive(part % 2, dz, dx)
+        seen.add((part, dz, dx))
+        if all((p, dz, i) in seen for p in (part // 2 * 2, part // 2 * 2 + 1) for i in range(NX)):
+            if part < 2:
+                projected += 1
+                for i in range(2):
+                    queue.append(lambda dz=dz, n=projected, i=i: project(dz, n == 1, n == NZ, i))
+                if projected == NZ:
+                    queue.extend(mixing())
+            else:
+                ready.add(dz)
+        if projected == NZ:
+            while chunk < NZ and ready >= set(CHUNKS[chunk][1]):
+                queue.append(lambda k=chunk: stages(k))
+                chunk += 1
+        for _ in range(1 if projected < NZ else 2):
+            if queue:
+                queue.pop(0)()
+    for piece in queue:
+        piece()
+    for k in range(NZ, NZ + 3):
+        stages(k)
+
     wg.finish()
     og.finish()
-    tail_copy.wait_send()
-    halo_copy.wait_send()
+    flight["tail"].wait_send()
+    flight["halo"].wait_send()
     for k in range(NZ):
         cs[k].wait_send()
         ys[k][0].wait_send()

time: 185 us -> 144 us (0.78)
  the two profiles are of different devices: /device:TPU:2 before, /device:TPU:1 now
where the time goes in v3:
time: 144 us; the launch traced here: 143 us
  Pallas kernels  140 us (97%)
  local copies, waits for them, and re-layouts  3.4 us (2%)
    pallas_call x1, Pallas kernels, per_device(): pl.pallas_call(kernel, out_shape=jax.ShapeDtypeStruct((block, depth), bf)...  140 us

profile of v3, /device:TPU:1, one launch (start us, length us, event | category | flops | bytes accessed | tf_op | source)
XLA Modules:
  0.0 143.0 jit_solution(17410576711843398510)
XLA Ops:
  0.0 1.3 copy.8.decay_ref
  1.3 139.6 %shard_map.73 = bf16[96,4096]{1,0:T(8,128)(2,1)} custom-call(bf16[768,4096]{1,0:T(8,128)(2,1)} %tokens_hbm.1, bf16[3,128,512]{2,1,0:T(8,128)(2,1)} %qkv_hbm.1, f32[3,7,512]{2,1,0:T(8,128)} %short_ref.1, f32[32,128]{1,0:T(8,128)} %long_ref.1, f32[32,1]{1,0:T(8,128)} %copy.8.decay_ref, f32[1,512]{1,0:T(1,128)} %bitcast.2, bf16[512,128]{1,0:T(8,128)(2,1)} %out_hbm.1), custom_call_target="tpu_custom_call" | custom-call | tf_op jit(solution)/shard_map/pallas_call | solution.py:392
  140.9 2.1 %copy.10 = bf16[96,4096]{1,0:T(8,128)(2,1)} copy(bf16[96,4096]{1,0:T(8,128)(2,1)} %shard_map.73) | data formatting | bytes 1572864

commit v4 on v3

--- a/solution.py
+++ b/solution.py
@@ -8,12 +8,13 @@
 MESH = pl.DeviceIdType.MESH
 NZ, NX, NY = 8, 4, 4
 ORDER = (
-    36, 60, 1, 3, 4, 28, 33, 35, 2, 40, 56, 5, 7, 8, 24, 37, 61, 29, 31, 39, 63, 34, 11, 44, 52,
-    6, 27, 12, 20, 9, 25, 41, 57, 43, 59, 15, 30, 38, 62, 13, 23, 48, 53, 21, 10, 55, 16, 26,
-    58, 45, 14, 47, 19, 42, 22, 54, 49, 17, 64, 51, 46, 124, 100, 67, 92, 99, 68, 18, 65, 120,
-    50, 97, 104, 88, 93, 95, 103, 127, 69, 71, 72, 116, 66, 101, 125, 98, 108, 91, 89, 84, 107,
-    75, 123, 94, 76, 70, 121, 105, 73, 126, 102, 87, 90, 119, 112, 117, 111, 79, 85, 77, 122,
-    80, 74, 109, 106, 115, 86, 118, 78, 113, 83, 110, 81, 114, 82,
+    4, 28, 33, 1, 36, 60, 200, 5, 8, 24, 29, 37, 61, 201, 9, 40, 56, 12, 20, 25, 41, 57, 64,
+    202, 13, 44, 52, 97, 300, 300, 99, 300, 300, 300, 16, 53, 21, 300, 98, 92, 300, 300, 45,
+    300, 68, 300, 300, 300, 300, 88, 48, 300, 300, 300, 17, 49, 301, 300, 72, 300, 300, 84, 300,
+    300, 300, 65, 67, 300, 100, 124, 93, 95, 300, 69, 71, 300, 101, 125, 89, 91, 300, 73, 75,
+    300, 103, 127, 85, 87, 66, 300, 102, 126, 94, 300, 70, 76, 120, 90, 300, 74, 104, 121, 86,
+    300, 105, 300, 123, 107, 300, 77, 79, 122, 300, 106, 300, 116, 80, 117, 108, 78, 119, 109,
+    118, 111, 81, 83, 300, 110, 300, 112, 300, 113, 115, 300, 82, 114, 300, 300, 300, 300, 300,
 )
 CHUNKS = ((0, (0,)), (1, (1, 7)), (7, (1, 7)), (2, (2, 6)), (6, (2, 6)), (3, (3, 5)), (5, (3, 5)), (4, (4,)))
 
@@ -22,77 +23,153 @@
     def __init__(self, place, slot, send_sem, recv_sem):
         self.z, self.x, self.step = place
         self.slot, self.send_sem, self.recv_sem = slot, send_sem, recv_sem
-        self.sent = []
+        self.sent, self.held = [], None
 
     def source(self, dz, dx):
         z = lax.rem(self.z - self.step * dz + NZ, NZ)
         x = lax.rem(self.x - self.step * dx + NX, NX)
         return z * NX + x
 
-    def copy(self, part, dz, dx, axis, way):
-        ref = self.slot(part, self.source(dz, dx))
+    def chip(self, axis, way):
         z, x = self.z, self.x
         if axis == "z":
-            z, dz = lax.rem(z + way * self.step + NZ, NZ), (dz + way) % NZ
+            z = lax.rem(z + way * self.step + NZ, NZ)
         else:
-            x, dx = lax.rem(x + way * self.step + NX, NX), (dx + way) % NX
+            x = lax.rem(x + way * self.step + NX, NX)
+        return z * NX + x
+
+    def reach(self, dz, dx, axis, way):
+        return ((dz + way) % NZ, dx) if axis == "z" else (dz, (dx + way) % NX)
+
+    def transfer(self, part, dz, dx, index, device):
+        ref = self.slot(part, self.source(dz, dx))
         return pltpu.make_async_remote_copy(
             src_ref=ref,
             dst_ref=ref,
-            send_sem=self.send_sem.at[part, dz, dx],
-            recv_sem=self.recv_sem.at[part, dz, dx],
-            device_id={"ctx": z * NX + x},
+            send_sem=self.send_sem.at[part, *index],
+            recv_sem=self.recv_sem.at[part, *index],
+            device_id={"ctx": device},
             device_id_type=MESH,
         )
 
-    def send(self, *args):
-        copy = self.copy(*args)
+    def send(self, part, dz, dx, axis, way):
+        index = self.reach(dz, dx, axis, way)
+        copy = self.transfer(part, dz, dx, index, self.chip(axis, way))
         copy.start()
         self.sent.append(copy)
 
     def wait(self, part, dz, dx):
         if (dz, dx) != (0, 0):
-            ref = self.slot(part, self.source(dz, dx))
-            pltpu.make_async_remote_copy(
-                src_ref=ref,
-                dst_ref=ref,
-                send_sem=self.send_sem.at[part, dz, dx],
-                recv_sem=self.recv_sem.at[part, dz, dx],
-                device_id={"ctx": lax.rem(self.z + 1, NZ) * NX + self.x},
-                device_id_type=MESH,
-            ).wait_recv()
+            self.transfer(part, dz, dx, (dz, dx), self.chip("z", 1)).wait_recv()
+
+    def along_z(self, part, dz, dx):
+        ways = [w for w, go in ((1, dz < NZ // 2), (-1, dz == 0 or dz > NZ // 2 + 1)) if go]
+        return [(part, dz, dx, "z", w) for w in ways]
+
+    def along_x(self, part, dz, dx):
+        ways = [w for w, go in ((1, dx < NX // 2), (-1, dx == 0 or dx > NX // 2 + 1)) if go]
+        return [(part, dz, dx, "x", w) for w in ways]
 
     def targets(self, part, dz, dx):
-        along_z = [w for w, go in ((1, dz < NZ // 2), (-1, dz == 0 or dz > NZ // 2 + 1)) if go]
-        along_x = [w for w, go in ((1, dx < NX // 2), (-1, dx == 0 or dx > NX // 2 + 1)) if go]
         if part == 0:
-            first = [(part, dz, dx, "x", w) for w in along_x]
-            return first, [(part, dz, dx, "z", w) for w in along_z] if dx == 0 else []
-        first = [(part, dz, dx, "z", w) for w in along_z]
-        return first, [(part, dz, dx, "x", w) for w in along_x] if dz == 0 else []
+            return self.along_z(part, dz, dx) if dx == 0 else [], self.along_x(part, dz, dx)
+        return self.along_x(part, dz, dx) if dz == 0 else [], self.along_z(part, dz, dx)
 
     def begin(self):
         both = [self.targets(part, 0, 0) for part in range(2)]
-        for target in [t for i in range(2) for pair in both for t in pair[i]]:
+        for target in [t for pair in both for t in pair[0]]:
             self.send(*target)
+        self.later([t for pair in both for t in pair[1]])
+
+    def later(self, targets):
+        if self.held is not None:
+            self.held.extend(targets)
+            return
+        for target in targets:
+            self.send(*target)
+
+    def release(self):
+        held, self.held = self.held, None
+        self.later(held)
 
     def arrive(self, part, dz, dx):
         self.wait(part, dz, dx)
         first, second = self.targets(part, dz, dx)
-        for target in first + second:
+        for target in first:
             self.send(*target)
+        self.later(second)
 
     def finish(self):
         for copy in self.sent:
             copy.wait_send()
 
 
+class PairGather(Gather):
+    def __init__(self, place, logical, slot, send_sem, recv_sem, partner, psend_sem, precv_sem):
+        super().__init__(place, slot, send_sem, recv_sem)
+        self.kind = logical
+        self.partner, self.psend_sem, self.precv_sem = partner, psend_sem, precv_sem
+
+    def near(self, x):
+        return x + 1 - 2 * lax.rem(x, 2)
+
+    def source(self, dz, dx, step=None, kind=None):
+        step = self.step if step is None else step
+        kind = self.kind if kind is None else kind
+        x = self.x if dx == 0 else self.near(self.x)
+        return lax.rem(self.z - step * dz + NZ, NZ) * NX + x + kind * (NX - 1 - 2 * x)
+
+    def chip(self, axis, way):
+        if axis == "z":
+            return super().chip(axis, way)
+        return self.z * NX + self.near(self.x)
+
+    def reach(self, dz, dx, axis, way):
+        return super().reach(dz, dx, axis, way) if axis == "z" else (dz, 1)
+
+    def along_x(self, part, dz, dx):
+        return [(part, dz, dx, "x", 1)] if dx == 0 else []
+
+    def across(self, part, dz, dx, source):
+        ref = self.slot(part, source)
+        return pltpu.make_async_remote_copy(
+            src_ref=ref,
+            dst_ref=ref,
+            send_sem=self.psend_sem.at[part, dz, dx],
+            recv_sem=self.precv_sem.at[part, dz, dx],
+            device_id=self.partner,
+            device_id_type=MESH,
+        )
+
+    def share(self, part, dz, dx):
+        copy = self.across(part, dz, dx, self.source(dz, dx))
+        copy.start()
+        self.sent.append(copy)
+
+    def begin(self):
+        super().begin()
+        for part in range(2):
+            self.share(part, 0, 0)
+
+    def arrive(self, part, dz, dx):
+        super().arrive(part, dz, dx)
+        self.share(part, dz, dx)
+
+    def complete(self, dz):
+        other = (NZ - dz) % NZ
+        for part in range(2):
+            for dx in range(2):
+                source = self.source(other, dx, -self.step, 1 - self.kind)
+                self.across(part, other, dx, source).wait_recv()
+
+
 def kernel(
-    tokens_hbm, qkv_hbm, short_ref, long_ref, decay_ref, gain_ref, out_hbm,
-    result_ref,
-    tok, wq, wo, acc, quer, gat, band, mix, mixp, own,
+    tokens_hbm, qkv_hbm, short_in, long_in, decay_in, gain_in, out_hbm,
+    result_ref, short_ref, long_ref, decay_ref, gain_ref,
+    tok, wq, wo, acc, quer, gat, band, mix, mixr, mixp, own,
     cs_send, cs_recv, fs, fr, ms, mr, js, jr, tail_send, tail_recv, halo,
     local_sem, wq_ss, wq_rs, wo_ss, wo_rs, cs_ss, cs_rs, y_ss, y_rs, halo_ss, halo_rs,
+    wp_ss, wp_rs, swap_ss, swap_rs, tok_ss, tok_rs, par_ss, par_rs, mix_ss, mix_rs,
 ):
     ctx, tp = lax.axis_index("ctx"), lax.axis_index("tp")
     z, x = lax.div(ctx, NX), lax.rem(ctx, NX)
@@ -105,14 +182,50 @@
     block = tcount // (2 * NY)
     half = NY * block
 
-    local = [pltpu.make_async_copy(qkv_hbm.at[i], wq.at[pl.ds(pl.multiple_of(ctx * share, share), share), pl.ds(i * width, width)], local_sem.at[i]) for i in range(3)]
-    local.append(pltpu.make_async_copy(out_hbm, wo.at[ctx], local_sem.at[3]))
-    local.append(pltpu.make_async_copy(tokens_hbm, tok, local_sem.at[4]))
-    for copy in local:
-        copy.start()
-
-    after = {"ctx": lax.rem(ctx + 1, count)}
+    side_of = lax.div(x, NX // 2)
+    kind = lax.rem(core + side_of, 2)
+    far = NX - 1 - x
+    seat = x + kind * (NX - 1 - 2 * x)
+    where = z * NX + seat
+
+    def holder(row, col):
+        other = lax.rem(lax.div(col, NX // 2) + side_of, 2)
+        return {
+            "ctx": row * NX + col + other * (NX - 1 - 2 * col),
+            "tp": y * 2 + lax.rem(side_of + other, 2),
+        }
+
+    def remote(src, dst, ss, rs, device):
+        return pltpu.make_async_remote_copy(src_ref=src, dst_ref=dst, send_sem=ss, recv_sem=rs, device_id=device, device_id_type=MESH)
+
+    mate = {"ctx": z * NX + far, "tp": y * 2 + 1 - core}
     partner = {"tp": tp + step}
+    params = ((short_in, short_ref), (long_in, long_ref), (decay_in, decay_ref), (gain_in, gain_ref))
+
+    def shard_slot(source, i):
+        return wq.at[pl.ds(pl.multiple_of(source * share, share), share), pl.ds(i * width, width)]
+
+    def local_shard(i):
+        return pltpu.make_async_copy(qkv_hbm.at[i], shard_slot(ctx, i), local_sem.at[i])
+
+    def local_param(i):
+        return pltpu.make_async_copy(*params[i], local_sem.at[5 + i])
+
+    local_tok = pltpu.make_async_copy(tokens_hbm, tok, local_sem.at[4])
+    local_out = pltpu.make_async_copy(out_hbm, wo.at[ctx], local_sem.at[3])
+
+    @pl.when(kind == 0)
+    def _():
+        for i in range(3):
+            local_shard(i).start()
+        for i in range(4):
+            local_param(i).start()
+        local_tok.start()
+
+    local_out.start()
+
+    after = holder(lax.rem(z + lax.div(seat + 1, NX), NZ), lax.rem(seat + 1, NX))
+    before = holder(lax.rem(z + NZ - 1 + lax.div(seat + NX - 1, NX), NZ), lax.rem(seat + NX - 1, NX))
     y_up = {"tp": lax.rem(y + step + NY, NY) * 2 + core}
     y_down = {"tp": lax.rem(y - step + NY, NY) * 2 + core}
     barrier = pltpu.get_barrier_semaphore()
@@ -122,7 +235,8 @@
         {"ctx": z * NX + lax.rem(x + 1, NX)},
         {"ctx": z * NX + lax.rem(x + NX - 1, NX)},
         after,
-        {"ctx": lax.rem(ctx + count - 1, count)},
+        before,
+        mate,
         partner,
         y_up,
         y_down,
@@ -131,8 +245,8 @@
         pl.semaphore_signal(barrier, inc=1, device_id=device, device_id_type=MESH)
     pl.semaphore_wait(barrier, len(neighbours))
 
-    cut = 7 * 128
-    ocut = 304
+    cut = 6 * 128
+    ocut = 208
 
     def wq_slot(part, source):
         rows = pl.ds(pl.multiple_of(source * share, share), share)
@@ -142,14 +256,79 @@
         return wo.at[source, pl.ds(0, ocut), :] if part == 0 else wo.at[source, pl.ds(ocut, width - ocut), :]
 
     place = (z, x, step)
-    wg = Gather(place, wq_slot, wq_ss, wq_rs)
+    wg = PairGather(place, kind, wq_slot, wq_ss, wq_rs, partner, wp_ss, wp_rs)
     og = Gather(place, wo_slot, wo_ss, wo_rs)
-
-    for copy in local[:3]:
-        copy.wait()
+    og.held = []
+
+    def swap_shard(i, source):
+        return remote(qkv_hbm.at[i], shard_slot(source, i), swap_ss.at[i], swap_rs.at[i], mate)
+
+    def share_param(i):
+        return remote(*params[i], par_ss.at[i], par_rs.at[i], partner)
+
+    quarter = tcount // NY
+    eighth = quarter // 2
+    opposite = lax.rem(y + 2, NY)
+
+    def token_rows(q, h, n):
+        return pl.ds(pl.multiple_of(q * quarter + h * eighth, 16), n)
+
+    def token_cross(i):
+        rows = token_rows(y, i, eighth) if i < 2 else token_rows(opposite, 0, quarter)
+        return remote(tokens_hbm.at[rows, :], tok.at[rows, :], tok_ss.at[i], tok_rs.at[i], mate)
+
+    def token_pass(h, way, q):
+        rows = token_rows(q, h, eighth)
+        i = 3 + 2 * h + (0 if way > 0 else 1)
+        to = {"tp": lax.rem(y + way + NY, NY) * 2 + core}
+        return remote(tok.at[rows, :], tok.at[rows, :], tok_ss.at[i], tok_rs.at[i], to)
+
+    def token_step(i):
+        @pl.when(kind == 1)
+        def _():
+            if i < 2:
+                token_cross(i).wait_recv()
+                token_pass(i, 1, y).start()
+                token_pass(i, -1, y).start()
+            else:
+                token_cross(2).wait_recv()
+                for h in range(2):
+                    for way in (1, -1):
+                        token_pass(h, way, lax.rem(y - way + NY, NY)).wait_recv()
+
+        if i == 2:
+            @pl.when(kind == 0)
+            def _():
+                local_tok.wait()
+
+    @pl.when(kind == 0)
+    def _():
+        for i in range(4):
+            share_param(i).start()
+        for i in range(3):
+            local_shard(i).wait()
+
+    @pl.when(kind == 1)
+    def _():
+        for i in range(3):
+            swap_shard(i, ctx).start()
+        for i in range(3):
+            token_cross(i).start()
+        for i in range(3):
+            swap_shard(i, where).wait_recv()
+
     wg.begin()
-    for copy in local[3:]:
-        copy.wait()
+    local_out.wait()
+
+    @pl.when(kind == 0)
+    def _():
+        for i in range(4):
+            local_param(i).wait()
+
+    @pl.when(kind == 1)
+    def _():
+        for i in range(4):
+            share_param(i).wait_recv()
 
     taps = long_ref.shape[1]
     lane = lax.broadcasted_iota(jnp.int32, (1, taps), 1).astype(jnp.float32)
@@ -173,7 +352,9 @@
     def project(dz, first, last, part_of):
         source = lax.rem(z - step * dz + NZ, NZ)
         rows = pl.ds(pl.multiple_of(source * span, span), span)
-        loops = 3 * width // tile // 2
+        loops = 3 * width // tile // 3
+        if part_of == 0:
+            wg.complete(dz)
 
         def one(n, carry):
             cols = pl.ds(pl.multiple_of((part_of * loops + n) * tile, tile), tile)
@@ -187,9 +368,6 @@
 
         lax.fori_loop(0, loops, one, 0)
 
-    def remote(src, dst, ss, rs, device):
-        return pltpu.make_async_remote_copy(src_ref=src, dst_ref=dst, send_sem=ss, recv_sem=rs, device_id=device, device_id_type=MESH)
-
     flight = {}
 
     def send_tail():
@@ -227,11 +405,11 @@
 
     def take_tail():
         flight["tail"].wait_recv()
-        acc[0:lead, :] = jnp.where(ctx > 0, tail_recv[...].astype(jnp.float32)[16 - lead :, :], 0.0)
+        acc[0:lead, :] = jnp.where(where > 0, tail_recv[...].astype(jnp.float32)[16 - lead :, :], 0.0)
 
     def take_halo():
         flight["halo"].wait_recv()
-        gat[0:taps, :] = jnp.where(ctx > 0, halo[...].astype(jnp.float32), 0.0).astype(jnp.bfloat16)
+        gat[0:taps, :] = jnp.where(where > 0, halo[...].astype(jnp.float32), 0.0).astype(jnp.bfloat16)
 
     group_of = lax.broadcasted_iota(jnp.int32, (taps, 2 * lanes), 1) % lanes // 16
     per_tile = lanes // 16
@@ -257,13 +435,33 @@
             mix[rows, cols] = (quer[rows, cols] * (total[:, h * lanes : (h + 1) * lanes] + gain * gated)).astype(jnp.bfloat16)
         return carry
 
+    def mix_copy(p):
+        rows = pl.ds(p * 2 * taps, 2 * taps)
+        return remote(mix.at[rows, :], mixr.at[rows, :], mix_ss.at[p], mix_rs.at[p], mate)
+
+    def send_mix(p):
+        @pl.when(kind == 1)
+        def _():
+            mix_copy(p).start()
+
     def order_rows():
-        for side in range(2):
-            ahead = -step if side == 0 else step
-            to_core = 1 - core if side == 0 else core
-            for j in range(NY):
-                to = lax.rem(y + ahead * j + NY, NY) * 2 + to_core
-                mixp[side * half + j * block : side * half + (j + 1) * block, :] = mix[pl.ds(pl.multiple_of(to * block, 16), block), :]
+        def fill(rows_from):
+            for side in range(2):
+                ahead = -step if side == 0 else step
+                to_core = 1 - core if side == 0 else core
+                for j in range(NY):
+                    to = lax.rem(y + ahead * j + NY, NY) * 2 + to_core
+                    mixp[side * half + j * block : side * half + (j + 1) * block, :] = rows_from[pl.ds(pl.multiple_of(to * block, 16), block), :]
+
+        @pl.when(kind == 0)
+        def _():
+            fill(mix)
+
+        @pl.when(kind == 1)
+        def _():
+            for p in range(blocks // 2):
+                mix_copy(p).wait_recv()
+            fill(mixr)
 
     def stage0(k):
         offset, needs = CHUNKS[k]
@@ -322,44 +520,58 @@
             stage3(k - 3)
 
     def mixing():
-        pairs = blocks // 2
+        def conv(p):
+            lax.fori_loop(p * tiles, (p + 1) * tiles, convolve, 0)
+            send_mix(p)
+
         yield send_tail
         yield lambda: (feature_rows(blocks - 1), send_halo())
         for r in range(blocks - 2, 0, -1):
             yield lambda r=r: feature_rows(r)
+            if r % 2 == 1:
+                yield lambda p=r // 2 + 1: conv(p)
         yield lambda: (take_tail(), feature_rows(0))
-        for p in range(pairs - 1, -1, -1):
-            if p == 0:
-                yield take_halo
-            yield lambda p=p: lax.fori_loop(p * tiles, p * tiles + tiles // 2, convolve, 0)
-            yield lambda p=p: lax.fori_loop(p * tiles + tiles // 2, (p + 1) * tiles, convolve, 0)
+        yield take_halo
+        yield lambda: conv(0)
         yield order_rows
 
     queue, seen, projected, chunk = [], {(p, 0, 0) for p in range(4)}, 0, 0
-    ready = set()
+    ready, tokens_in = set(), False
+    waiting = [0, 1, 7, 2, 6, 3, 5, 4]
     for code in ORDER:
-        part, dz, dx = code // 32, code % 32 // 4, code % 4
         if code == 64:
             og.begin()
             continue
-        (wg if part < 2 else og).arrive(part % 2, dz, dx)
-        seen.add((part, dz, dx))
-        if all((p, dz, i) in seen for p in (part // 2 * 2, part // 2 * 2 + 1) for i in range(NX)):
-            if part < 2:
-                projected += 1
-                for i in range(2):
-                    queue.append(lambda dz=dz, n=projected, i=i: project(dz, n == 1, n == NZ, i))
-                if projected == NZ:
-                    queue.extend(mixing())
-            else:
+        if code == 301:
+            og.release()
+            continue
+        if code == 300:
+            queue.pop(0)()
+            continue
+        if code >= 200:
+            token_step(code - 200)
+            tokens_in = code == 202
+        else:
+            part, dz, dx = code // 32, code % 32 // 4, code % 4
+            (wg if part < 2 else og).arrive(part % 2, dz, dx)
+            seen.add((part, dz, dx))
+            if part >= 2 and all((p, dz, i) in seen for p in (2, 3) for i in range(NX)):
                 ready.add(dz)
+        while tokens_in and waiting:
+            dz = waiting[0]
+            twins = (dz, (NZ - dz) % NZ)
+            if not all((p, d, i) in seen for p in (0, 1) for d in twins for i in range(2)):
+                break
+            waiting.pop(0)
+            projected += 1
+            for i in range(3):
+                queue.append(lambda dz=dz, n=projected, i=i: project(dz, n == 1, n == NZ, i))
+            if projected == NZ:
+                queue.extend(mixing())
         if projected == NZ:
             while chunk < NZ and ready >= set(CHUNKS[chunk][1]):
                 queue.append(lambda k=chunk: stages(k))
                 chunk += 1
-        for _ in range(1 if projected < NZ else 2):
-            if queue:
-                queue.pop(0)()
     for piece in queue:
         piece()
     for k in range(NZ, NZ + 3):
@@ -374,6 +586,21 @@
         ys[k][0].wait_send()
         ys[k][1].wait_send()
         jn[k].wait_send()
+
+    @pl.when(kind == 0)
+    def _():
+        for i in range(4):
+            share_param(i).wait_send()
+
+    @pl.when(kind == 1)
+    def _():
+        for i in range(3):
+            swap_shard(i, ctx).wait_send()
+            token_cross(i).wait_send()
+            mix_copy(i).wait_send()
+        for h in range(2):
+            token_pass(h, 1, y).wait_send()
+            token_pass(h, -1, y).wait_send()
 
 
 def per_device(tokens, qkv_weight, short_filter, long_filter, decay_rate, skip_gain, out_weight):
@@ -395,6 +622,10 @@
         in_specs=[any_spec, any_spec, vmem, vmem, vmem, vmem, any_spec],
         out_specs=vmem,
         scratch_shapes=[
+            pltpu.VMEM(short_filter.shape, f32),
+            pltpu.VMEM(long_filter.shape, f32),
+            pltpu.VMEM((groups, 1), f32),
+            pltpu.VMEM((1, width), f32),
             pltpu.VMEM((tcount, depth), bf),
             pltpu.VMEM((depth, 3 * width), bf),
             pltpu.VMEM((NZ * NX, width, share), bf),
@@ -404,6 +635,7 @@
             pltpu.VMEM((groups * taps, 2 * taps), bf),
             pltpu.VMEM((tcount, width), bf),
             pltpu.VMEM((tcount, width), bf),
+            pltpu.VMEM((tcount, width), bf),
             pltpu.VMEM((4, half, span), f32),
             pltpu.VMEM((NZ, half, span), bf),
             pltpu.VMEM((NZ, half, span), bf),
@@ -411,9 +643,9 @@
             pltpu.VMEM((16, 3 * width), bf),
             pltpu.VMEM((16, 3 * width), bf),
             pltpu.VMEM((taps, width), bf),
-            dma((5,)),
-            dma((2, NZ, NX)),
-            dma((2, NZ, NX)),
+            dma((9,)),
+            dma((2, NZ, 2)),
+            dma((2, NZ, 2)),
             dma((2, NZ, NX)),
             dma((2, NZ, NX)),
             dma((NZ,)),
@@ -422,6 +654,16 @@
             dma((3, NZ)),
             dma((2,)),
             dma((2,)),
+            dma((2, NZ, 2)),
+            dma((2, NZ, 2)),
+            dma((3,)),
+            dma((3,)),
+            dma((7,)),
+            dma((7,)),
+            dma((4,)),
+            dma((4,)),
+            dma((3,)),
+            dma((3,)),
         ],
         compiler_params=pltpu.CompilerParams(
             collective_id=0, has_side_effects=True, vmem_limit_bytes=67043328

time: 144 us -> 131 us (0.910)
  Pallas kernels: 140 us -> 126 us
    pallas_call x1, Pallas kernels: 140 us -> 126 us  [per_device(): pl.pallas_call(kernel, out_shape=jax.ShapeDtypeStruct((block, depth), bf)...]
where the time goes in v4:
time: 131 us; the launch traced here: 129 us
  Pallas kernels  126 us (96%)
  local copies, waits for them, and re-layouts  3.4 us (3%)
    pallas_call x1, Pallas kernels, per_device(): pl.pallas_call(kernel, out_shape=jax.ShapeDtypeStruct((block, depth), bf)...  126 us

profile of v4, /device:TPU:1, one launch (start us, length us, event | category | flops | bytes accessed | tf_op | source)
XLA Modules:
  0.0 129.3 jit_solution(4856176192925117605)
XLA Ops:
  0.0 1.3 %copy.8.decay_in = f32[32,1]{1,0:T(8,128)} copy(f32[32,1]{0,1:T(1,128)} %bitcast.3) | data formatting | bytes 256 | tf_op jit(solution)/shard_map/broadcast_in_dim | solution.py:676
  1.3 125.9 %shard_map.73 = bf16[96,4096]{1,0:T(8,128)(2,1)} custom-call(bf16[768,4096]{1,0:T(8,128)(2,1)} %tokens_hbm.1, bf16[3,128,512]{2,1,0:T(8,128)(2,1)} %qkv_hbm.1, f32[3,7,512]{2,1,0:T(8,128)} %short_in.1, f32[32,128]{1,0:T(8,128)} %long_in.1, f32[32,1]{1,0:T(8,128)} %copy.8.decay_in, f32[1,512]{1,0:T(1,128)} %bitcast.2, bf16[512,128]{1,0:T(8,128)(2,1)} %out_hbm.1), custom_call_target="tpu_custom_call" | custom-call | tf_op jit(solution)/shard_map/pallas_call | solution.py:619
  127.3 2.1 %copy.10 = bf16[96,4096]{1,0:T(8,128)(2,1)} copy(bf16[96,4096]{1,0:T(8,128)(2,1)} %shard_map.73) | data formatting | bytes 1572864

commit v5 on v4

--- a/solution.py
+++ b/solution.py
@@ -8,13 +8,14 @@
 MESH = pl.DeviceIdType.MESH
 NZ, NX, NY = 8, 4, 4
 ORDER = (
-    4, 28, 33, 1, 36, 60, 200, 5, 8, 24, 29, 37, 61, 201, 9, 40, 56, 12, 20, 25, 41, 57, 64,
-    202, 13, 44, 52, 97, 300, 300, 99, 300, 300, 300, 16, 53, 21, 300, 98, 92, 300, 300, 45,
-    300, 68, 300, 300, 300, 300, 88, 48, 300, 300, 300, 17, 49, 301, 300, 72, 300, 300, 84, 300,
-    300, 300, 65, 67, 300, 100, 124, 93, 95, 300, 69, 71, 300, 101, 125, 89, 91, 300, 73, 75,
-    300, 103, 127, 85, 87, 66, 300, 102, 126, 94, 300, 70, 76, 120, 90, 300, 74, 104, 121, 86,
-    300, 105, 300, 123, 107, 300, 77, 79, 122, 300, 106, 300, 116, 80, 117, 108, 78, 119, 109,
-    118, 111, 81, 83, 300, 110, 300, 112, 300, 113, 115, 300, 82, 114, 300, 300, 300, 300, 300,
+    4, 28, 33, 200, 1, 36, 60, 201, 5, 8, 24, 202, 29, 37, 61, 203, 9, 40, 56, 12, 20, 25, 41,
+    57, 64, 204, 13, 44, 52, 300, 300, 300, 300, 97, 300, 99, 300, 16, 53, 21, 300, 300, 300,
+    300, 45, 92, 300, 300, 300, 300, 68, 98, 48, 300, 300, 300, 17, 300, 300, 49, 301, 300, 88,
+    300, 72, 300, 300, 300, 300, 300, 300, 300, 65, 67, 300, 100, 124, 93, 95, 69, 71, 300, 101,
+    125, 89, 91, 300, 73, 75, 103, 127, 300, 300, 102, 126, 66, 300, 76, 84, 300, 94, 104, 120,
+    70, 90, 105, 121, 74, 107, 123, 300, 77, 79, 106, 122, 85, 87, 80, 300, 108, 116, 300, 109,
+    117, 300, 111, 119, 78, 83, 86, 300, 110, 118, 81, 112, 300, 113, 300, 115, 300, 114, 82,
+    300,
 )
 CHUNKS = ((0, (0,)), (1, (1, 7)), (7, (1, 7)), (2, (2, 6)), (6, (2, 6)), (3, (3, 5)), (5, (3, 5)), (4, (4,)))
 
@@ -267,36 +268,49 @@
         return remote(*params[i], par_ss.at[i], par_rs.at[i], partner)
 
     quarter = tcount // NY
-    eighth = quarter // 2
+    part_rows = quarter // 4
     opposite = lax.rem(y + 2, NY)
 
     def token_rows(q, h, n):
-        return pl.ds(pl.multiple_of(q * quarter + h * eighth, 16), n)
+        return pl.ds(pl.multiple_of(q * quarter + h * part_rows, 16), n)
 
     def token_cross(i):
-        rows = token_rows(y, i, eighth) if i < 2 else token_rows(opposite, 0, quarter)
+        rows = token_rows(y, i, part_rows) if i < 4 else token_rows(opposite, 2, 2 * part_rows)
         return remote(tokens_hbm.at[rows, :], tok.at[rows, :], tok_ss.at[i], tok_rs.at[i], mate)
 
-    def token_pass(h, way, q):
-        rows = token_rows(q, h, eighth)
-        i = 3 + 2 * h + (0 if way > 0 else 1)
+    def along_y(rows, i, way):
         to = {"tp": lax.rem(y + way + NY, NY) * 2 + core}
         return remote(tok.at[rows, :], tok.at[rows, :], tok_ss.at[i], tok_rs.at[i], to)
+
+    def token_pass(h, way, q):
+        return along_y(token_rows(q, h, part_rows), 5 + 2 * h + (way < 0), way)
+
+    def token_relay(way, q):
+        return along_y(token_rows(q, int(way > 0), part_rows), 13 + (way < 0), way)
+
+    def from_side(way):
+        return lax.rem(y - way + NY, NY)
 
     def token_step(i):
         @pl.when(kind == 1)
         def _():
-            if i < 2:
+            if i < 4:
                 token_cross(i).wait_recv()
                 token_pass(i, 1, y).start()
                 token_pass(i, -1, y).start()
+                if i >= 2:
+                    way = -1 if i == 2 else 1
+                    token_pass(i - 2, way, from_side(way)).wait_recv()
+                    token_relay(way, from_side(way)).start()
             else:
-                token_cross(2).wait_recv()
-                for h in range(2):
-                    for way in (1, -1):
-                        token_pass(h, way, lax.rem(y - way + NY, NY)).wait_recv()
-
-        if i == 2:
+                token_cross(4).wait_recv()
+                for way in (1, -1):
+                    for h in range(4):
+                        if (h, way) not in ((0, -1), (1, 1)):
+                            token_pass(h, way, from_side(way)).wait_recv()
+                    token_relay(way, opposite).wait_recv()
+
+        if i == 4:
             @pl.when(kind == 0)
             def _():
                 local_tok.wait()
@@ -312,7 +326,7 @@
     def _():
         for i in range(3):
             swap_shard(i, ctx).start()
-        for i in range(3):
+        for i in range(5):
             token_cross(i).start()
         for i in range(3):
             swap_shard(i, where).wait_recv()
@@ -332,11 +346,13 @@
 
     taps = long_ref.shape[1]
     lane = lax.broadcasted_iota(jnp.int32, (1, taps), 1).astype(jnp.float32)
+    group_id = lax.broadcasted_iota(jnp.int32, decay_ref.shape, 1)
     row_id = lax.broadcasted_iota(jnp.int32, (taps, taps), 0)
     col_id = lax.broadcasted_iota(jnp.int32, (taps, taps), 1)
 
     def build(group, carry):
-        filt = long_ref[pl.ds(group, 1), :] * jnp.exp(-decay_ref[pl.ds(group, 1), :] * lane)
+        rate = jnp.sum(jnp.where(group_id == group, decay_ref[...], 0.0), axis=1, keepdims=True)
+        filt = long_ref[pl.ds(group, 1), :] * jnp.exp(-rate * lane)
         ring = pltpu.roll(jnp.broadcast_to(filt, (taps, taps)), 0, 1, stride=1, stride_axis=0).T
         rows = pl.ds(pl.multiple_of(group * taps, taps), taps)
         band[rows, 0:taps] = jnp.where(col_id > row_id, ring, 0.0).astype(jnp.bfloat16)
@@ -550,7 +566,7 @@
             continue
         if code >= 200:
             token_step(code - 200)
-            tokens_in = code == 202
+            tokens_in = code == 204
         else:
             part, dz, dx = code // 32, code % 32 // 4, code % 4
             (wg if part < 2 else og).arrive(part % 2, dz, dx)
@@ -596,11 +612,13 @@
     def _():
         for i in range(3):
             swap_shard(i, ctx).wait_send()
+            mix_copy(i).wait_send()
+        for i in range(5):
             token_cross(i).wait_send()
-            mix_copy(i).wait_send()
-        for h in range(2):
-            token_pass(h, 1, y).wait_send()
-            token_pass(h, -1, y).wait_send()
+        for way in (1, -1):
+            for h in range(4):
+                token_pass(h, way, y).wait_send()
+            token_relay(way, from_side(way)).wait_send()
 
 
 def per_device(tokens, qkv_weight, short_filter, long_filter, decay_rate, skip_gain, out_weight):
@@ -624,7 +642,7 @@
         scratch_shapes=[
             pltpu.VMEM(short_filter.shape, f32),
             pltpu.VMEM(long_filter.shape, f32),
-            pltpu.VMEM((groups, 1), f32),
+            pltpu.VMEM((1, groups), f32),
             pltpu.VMEM((1, width), f32),
             pltpu.VMEM((tcount, depth), bf),
             pltpu.VMEM((depth, 3 * width), bf),
@@ -658,8 +676,8 @@
             dma((2, NZ, 2)),
             dma((3,)),
             dma((3,)),
-            dma((7,)),
-            dma((7,)),
+            dma((15,)),
+            dma((15,)),
             dma((4,)),
             dma((4,)),
             dma((3,)),
@@ -673,7 +691,7 @@
         qkv_weight,
         short_filter,
         long_filter,
-        decay_rate[:, None],
+        decay_rate[None, :],
         skip_gain[None, :],
         out_weight,
     )

time: 131 us -> 128 us (0.977)
  Pallas kernels: 126 us -> 124 us
  local copies, waits for them, and re-layouts: 3.4 us -> 2.06 us
    pallas_call x1, Pallas kernels: 126 us -> 124 us  [per_device(): pl.pallas_call(kernel, out_shape=jax.ShapeDtypeStruct((block, depth), bf)...]
    broadcast_in_dim x1 -> x0, local copies, waits for them, and re-layouts: 1.34 us -> none  [per_device(): decay_rate[:, None]]
where the time goes in v5:
time: 128 us; the launch traced here: 126 us
  Pallas kernels  124 us (97%)
  local copies, waits for them, and re-layouts  2.06 us (2%)
    pallas_call x1, Pallas kernels, per_device(): pl.pallas_call(kernel, out_shape=jax.ShapeDtypeStruct((block, depth), bf)...  124 us

profile of v5, /device:TPU:1, one launch (start us, length us, event | category | flops | bytes accessed | tf_op | source)
XLA Modules:
  0.0 126.5 jit_solution(14052503795635480752)
XLA Ops:
  0.0 124.4 %shard_map.73 = bf16[96,4096]{1,0:T(8,128)(2,1)} custom-call(bf16[768,4096]{1,0:T(8,128)(2,1)} %tokens_hbm.1, bf16[3,128,512]{2,1,0:T(8,128)(2,1)} %qkv_hbm.1, f32[3,7,512]{2,1,0:T(8,128)} %short_in.1, f32[32,128]{1,0:T(8,128)} %long_in.1, f32[1,32]{1,0:T(1,128)} %bitcast.3, f32[1,512]{1,0:T(1,128)} %bitcast.2, bf16[512,128]{1,0:T(8,128)(2,1)} %out_hbm.1), custom_call_target="tpu_custom_call" | custom-call | tf_op jit(solution)/shard_map/pallas_call | solution.py:637
  124.4 2.1 %copy.9 = bf16[96,4096]{1,0:T(8,128)(2,1)} copy(bf16[96,4096]{1,0:T(8,128)(2,1)} %shard_map.73) | data formatting | bytes 1572864
